TPU v7x, 32 devices: a whole 2x2x4 slice. The times are simulated.
32 devices in a mesh: groups: 2 (over x), gx: 16 (over z, y, core).
Axes of the slice: x: 2, y: 2, z: 4, core: 2. Of those that a mesh axis runs over, the one named last changes fastest.
Arguments:
- hidden: bfloat16 [39936, 768], P('gx', 'groups'), parts along dimension 1, may hold values from -6 to 6
- residual: bfloat16 [16384, 768], P('gx', 'groups'), parts along dimension 1, may hold values from -120 to 120
- w_down: bfloat16 [16, 19968, 2048], P('gx'), may hold values from -0.03125 to 0.03125
- gain: bfloat16 [16384], P('gx'), may hold values from 0.099609375 to 1.8984375
- w_qkv: bfloat16 [16, 2048, 5120], P('gx'), may hold values from -0.046875 to 0.046875
Outputs:
- stream: bfloat16 [16384, 768], P('gx', 'groups'), parts along dimension 1
- qkv: bfloat16 [10240, 768], P('gx', 'groups'), parts along dimension 1
There are 2 independent parts, one for each index of `groups`. A program takes and returns all parts, laid end to end along the dimension named above; an argument that names none is the same for every part. Nothing has to cross between parts.
All inputs are finite; a program needn't handle non-finite values.
Results may differ from a plain program's by a relative error of at most 0.0058.
Values may be sent and summed in bfloat16 or wider, within the bound.
No kernel may reach another device: no remote copies, remote signals or barrier semaphores. Data moves between devices by JAX's collectives and lax.ppermute only.
A program may use at most 192 MiB of HBM per device.

v0:
```python
import jax
import jax.numpy as jnp
from jax import lax
from jax.experimental import pallas as pl
from jax.experimental.pallas import tpu as pltpu
from jax.sharding import PartitionSpec as P


D = 16384
XS = 8
FAR = XS // 2
LANES = 128
ROOM = 8


IN_VMEM = pl.BlockSpec(memory_space=pltpu.VMEM)
IN_SMEM = pl.BlockSpec(memory_space=pltpu.SMEM)


def block_at(place):
    return jnp.where(place < FAR, 2 * place, 2 * (XS - 1 - place) + 1)


def place_of(block):
    return jnp.where(block % 2 == 0, block // 2, XS - 1 - block // 2)


def static_block_at(place):
    return 2 * place if place < FAR else 2 * (XS - 1 - place) + 1


def moved(value, ys, by):
    route = []
    for place in range(XS):
        source = static_block_at(place)
        target = static_block_at((place + by) % XS)
        for low in range(ys):
            route.append((source * ys + low, target * ys + low))
    return lax.ppermute(value, "gx", route)


def swapped(value, stride):
    count = lax.axis_size("gx")
    return lax.ppermute(value, "gx", [(low, low ^ 1 << stride) for low in range(count)])


def token_groups(tokens):
    if tokens % (3 * LANES):
        return [(0, tokens)]
    return [(0, tokens * 2 // 3), (tokens * 2 // 3, tokens)]


def down_step(table, acc, low, sides, tiles):
    count, groups = len(sides), len(sides[0][0])
    rows, width = tiles.shape[1:]
    widths = [piece.shape[1] for piece in sides[0][0]]
    size = sum(widths)
    block = min(width, 512)

    def body(table_ref, *refs):
        pieces, weights = refs[: count * groups], refs[count * groups : count * (groups + 1)]
        out, turned = refs[-2:]

        @pl.when(pl.program_id(0) == 0)
        def _():
            for j in range(count):
                start = 0
                for g in range(groups):
                    turned[j, start : start + widths[g], :] = pieces[j * groups + g][...].T
                    start += widths[g]

        total = None if acc is None else refs[count * (groups + 1)][...]
        for j in range(count):
            term = jnp.dot(turned[j], weights[j][0], preferred_element_type=jnp.float32)
            total = term if total is None else total + term
        out[...] = total

    def piece_spec(tokens):
        return pl.BlockSpec((rows, tokens), lambda i, table: (0, 0), pipeline_mode=pl.Buffered(1))

    def weight_spec(distance):
        at = distance % XS
        return pl.BlockSpec((1, rows, block), lambda i, table: (table[at], 0, i))

    in_specs = [piece_spec(tokens) for _ in sides for tokens in widths]
    in_specs += [weight_spec(far) for _, far in sides]
    operands = [piece for pieces, _ in sides for piece in pieces] + [tiles] * count
    if acc is not None:
        in_specs.append(pl.BlockSpec((size, block), lambda i, table: (low // size, i)))
        operands.append(acc)
    need = count * (4 * rows * size + 4 * rows * block) + 20 * size * block
    return pl.pallas_call(
        body,
        grid_spec=pltpu.PrefetchScalarGridSpec(
            num_scalar_prefetch=1,
            grid=(width // block,),
            in_specs=in_specs,
            out_specs=pl.BlockSpec((size, block), lambda i, table: (0, i)),
            scratch_shapes=[pltpu.VMEM((count, size, rows), jnp.bfloat16)],
        ),
        out_shape=jax.ShapeDtypeStruct((size, width), jnp.float32),
        name="down_step",
        compiler_params=pltpu.CompilerParams(vmem_limit_bytes=need + (1 << 20)),
        cost_estimate=pl.CostEstimate(
            flops=2 * count * rows * size * width,
            bytes_accessed=2 * count * rows * (size + width) + 8 * size * width,
            transcendentals=0,
        ),
    )(table, *operands)


def last_step(acc, pieces, weights, out_type):
    count = len(pieces)
    size, width = acc.shape
    block = min(width, 512)

    def body(*refs):
        piece_refs, weight_refs = refs[:count], refs[count : 2 * count]
        total_ref, out = refs[2 * count :]
        turned = [piece[...].T for piece in piece_refs]
        for at in range(0, width, block):
            columns = slice(at, at + block)
            total = total_ref[:, columns]
            for rows, weight in zip(turned, weight_refs):
                total = total + jnp.dot(
                    rows, weight[:, columns], preferred_element_type=jnp.float32
                )
            out[:, columns] = total.astype(out.dtype)

    flops = 2 * size * width * sum(piece.shape[0] for piece in pieces)
    return small_call(
        body,
        list(pieces) + list(weights) + [acc],
        jax.ShapeDtypeStruct((size, width), out_type),
        flops,
        limit=8,
    )


def token_slice(hidden, low, high):
    if low == 0 and high == hidden.shape[1]:
        return hidden

    parts = 8 if hidden.shape[0] % 64 == 0 else 1
    rows = hidden.shape[0] // parts

    def body(source, target, semaphores):
        copies = [
            pltpu.make_async_copy(
                source.at[j * rows : (j + 1) * rows, low:high],
                target.at[j * rows : (j + 1) * rows],
                semaphores.at[j],
            )
            for j in range(parts)
        ]
        for copy in copies:
            copy.start()
        for copy in copies:
            copy.wait()

    shape = (hidden.shape[0], high - low)
    return pl.pallas_call(
        body,
        in_specs=[pl.BlockSpec(memory_space=pltpu.HBM)],
        out_specs=IN_VMEM,
        out_shape=pltpu.VMEM(shape, hidden.dtype),
        scratch_shapes=[pltpu.SemaphoreType.DMA((parts,))],
        name="token_slice",
        compiler_params=pltpu.CompilerParams(vmem_limit_bytes=4 << 20),
        cost_estimate=pl.CostEstimate(
            flops=0, bytes_accessed=4 * shape[0] * shape[1], transcendentals=0
        ),
    )(pltpu.with_memory_space_constraint(hidden, pltpu.HBM))


def regrouped(table, source, picks, shape, pick_of):
    count = len(picks)

    def body(table_ref, source_ref, *refs):
        targets = refs[:count]
        buffers, arrive, leave = refs[count:]

        def load(j):
            block = source_ref.at[pick_of(table_ref, picks[j])]
            return pltpu.make_async_copy(block, buffers.at[j % 3], arrive.at[j % 3])

        def store(j):
            return pltpu.make_async_copy(buffers.at[j % 3], targets[j], leave.at[j % 3])

        for j in range(min(2, count)):
            load(j).start()
        for j in range(count):
            load(j).wait()
            store(j).start()
            if j + 2 < count:
                if j >= 1:
                    store(j - 1).wait()
                load(j + 2).start()
        for j in range(max(0, count - 3), count):
            store(j).wait()

    in_hbm = pl.BlockSpec(memory_space=pltpu.HBM)
    elements = count
    for extent in shape:
        elements *= extent
    return pl.pallas_call(
        body,
        in_specs=[IN_SMEM, in_hbm],
        out_specs=[in_hbm] * count,
        out_shape=[pltpu.HBM(shape, source.dtype)] * count,
        scratch_shapes=[
            pltpu.VMEM((3,) + shape, source.dtype),
            pltpu.SemaphoreType.DMA((3,)),
            pltpu.SemaphoreType.DMA((3,)),
        ],
        name="regrouped",
        compiler_params=pltpu.CompilerParams(vmem_limit_bytes=20 << 20),
        cost_estimate=pl.CostEstimate(flops=0, bytes_accessed=4 * elements, transcendentals=0),
    )(table, pltpu.with_memory_space_constraint(source, pltpu.HBM))


def small_call(body, operands, outs, flops, scratch=(), smem=0, limit=5):
    total = sum(x.size * x.dtype.itemsize for x in operands[smem:])
    single = not isinstance(outs, (list, tuple))
    return pl.pallas_call(
        body,
        in_specs=[IN_SMEM] * smem + [IN_VMEM] * (len(operands) - smem),
        out_specs=IN_VMEM if single else [IN_VMEM] * len(outs),
        out_shape=outs,
        scratch_shapes=list(scratch),
        compiler_params=pltpu.CompilerParams(vmem_limit_bytes=limit << 20),
        cost_estimate=pl.CostEstimate(flops=flops, bytes_accessed=total, transcendentals=0),
    )(*operands)


def finish(mine, theirs, res_t, low, gain_row, weights, columns, carry):
    size, width = mine.shape
    step = 16
    extra = ROOM if carry else 0

    def body(a, b, r, g, w, block, scaled, squares, shard, sums):
        @pl.loop(0, size // step, unroll=2)
        def _(i):
            rows = pl.ds(pl.multiple_of(i * step, step), step)
            res_rows = pl.ds(pl.multiple_of(i * step + low, step), step)
            both = a[rows, :].astype(jnp.float32) + b[rows, :].astype(jnp.float32)
            new = (r[res_rows, :].astype(jnp.float32) + both).astype(jnp.bfloat16)
            block[rows, :] = new
            value = new.astype(jnp.float32)
            scaled[rows, :] = (value * g[...]).astype(jnp.bfloat16)
            square = value * value
            sums[rows, :] = jnp.broadcast_to(
                jnp.sum(square, axis=1, keepdims=True), (step, LANES)
            )

        squares[...] = sums[...].T[:8]
        term = jnp.dot(scaled[...], w[...], preferred_element_type=jnp.float32)
        shard[:size, :] = term.astype(jnp.bfloat16)
        if carry:
            shard[size:, :] = carried(squares[...], columns)

    shapes = [
        jax.ShapeDtypeStruct((size, width), jnp.bfloat16),
        jax.ShapeDtypeStruct((size, width), jnp.bfloat16),
        jax.ShapeDtypeStruct((8, size), jnp.float32),
    ]
    shapes.append(pltpu.VMEM((size + extra, columns), jnp.bfloat16))
    return small_call(
        body,
        [mine, theirs, res_t, gain_row, weights],
        shapes,
        2 * size * width * columns,
        [pltpu.VMEM((size, LANES), jnp.float32)],
    )


def carried(total, columns):
    missing = columns - total.shape[1]
    if missing:
        total = jnp.concatenate([total, jnp.zeros((ROOM, missing), jnp.float32)], 1)
    high = total.astype(jnp.bfloat16).astype(jnp.float32)
    upper = lax.broadcasted_iota(jnp.int32, total.shape, 0) < ROOM // 2
    return jnp.where(upper, high, total - high).astype(jnp.bfloat16)


def uncarried(rows, count):
    both = rows.astype(jnp.float32)
    return (both + pltpu.roll(both, ROOM // 2, 0))[:, :count]


def hop(came, scaled, weights, squares, columns, carry):
    count = scaled.shape[0]
    first = came is None

    def body(*refs):
        came_ref = None if first else refs[0]
        x, w, q, out = refs[0 if first else 1 :]
        total = jnp.dot(x[...], w[...], preferred_element_type=jnp.float32)
        if not first:
            total = total + came_ref[:count, :].astype(jnp.float32)
        out[:count, :] = total.astype(jnp.bfloat16)
        if carry:
            sums = q[...]
            if not first:
                sums = sums + uncarried(came_ref[count:, :], count)
            out[count:, :] = carried(sums, columns)

    operands = ([] if first else [came]) + [scaled, weights, squares]
    shape = pltpu.VMEM((count + (ROOM if carry else 0), columns), jnp.bfloat16)
    return small_call(body, operands, shape, 2 * count * scaled.shape[1] * columns)


def own_term(scaled, weights, columns):
    def body(x, w, out):
        out[...] = jnp.dot(
            x[...], w[...], preferred_element_type=jnp.float32
        )

    size, width = scaled.shape
    shape = jax.ShapeDtypeStruct((size, columns), jnp.float32)
    return small_call(body, [scaled, weights], shape, 2 * size * width * columns)


def own_rows(low_index, blocks, own_width):
    def body(low_ref, *refs):
        at = pl.multiple_of(low_ref[0] * own_width, own_width)
        start = 0
        for ref in refs[:-1]:
            refs[-1][:, start : start + ref.shape[0]] = ref[:, pl.ds(at, own_width)].T
            start += ref.shape[0]

    tokens = sum(block.shape[0] for block in blocks)
    shape = jax.ShapeDtypeStruct((own_width, tokens), blocks[0].dtype)
    return small_call(body, [low_index.reshape(1)] + blocks, shape, 0, (), 1)


def last_sum(parts, carry):
    bounds = [0]
    for own, _, _, _ in parts:
        bounds.append(bounds[-1] + own.shape[0])
    tokens, columns = bounds[-1], parts[0][0].shape[1]

    def body(*refs):
        out, whole, sums = refs[-3:]
        for i, (low, high) in enumerate(zip(bounds, bounds[1:])):
            own, q, first, second = refs[4 * i : 4 * i + 4]
            count = high - low
            total = own[...] + first[:count, :].astype(jnp.float32)
            whole[low:high, :] = total + second[:count, :].astype(jnp.float32)
            square = q[...]
            if carry:
                square = square + uncarried(first[count:, :], count)
                square = square + uncarried(second[count:, :], count)
            sums[:, low:high] = square
        inverse = lax.rsqrt(sums[0:1, :] / D + 1e-05)
        out[...] = (whole[...].T * inverse).astype(jnp.bfloat16)

    return small_call(
        body,
        [array for part in parts for array in part],
        jax.ShapeDtypeStruct((columns, tokens), jnp.bfloat16),
        tokens * columns,
        [pltpu.VMEM((tokens, columns), jnp.float32), pltpu.VMEM((8, tokens), jnp.float32)],
    )


def on_device(hidden, residual, w_down, gain, w_qkv):
    dev_index = lax.axis_index("gx")
    ys = lax.axis_size("gx") // XS
    y_bits = ys.bit_length() - 1
    x_bits = XS.bit_length() - 1
    place = place_of(dev_index // ys)
    low_index = dev_index % ys
    table = block_at((place + jnp.arange(XS, dtype=jnp.int32)) % XS).astype(jnp.int32)

    chunk_rows, tokens = hidden.shape
    half_rows = chunk_rows // 2
    width = w_down.shape[2]
    own_width = residual.shape[0]
    columns = w_qkv.shape[2] // XS
    chunk_tiles = w_down.reshape(XS, chunk_rows, width)
    half_tiles = w_down.reshape(XS * 2, half_rows, width)
    qkv_tile = w_qkv[0]
    if columns % LANES:
        qkv_tile = qkv_tile.reshape(width, XS, columns).transpose(1, 0, 2)

    bounds = token_groups(tokens)

    ups, downs = [], []
    for low, high in bounds:
        own = token_slice(hidden, low, high)
        up, down = [own], [own]
        for step in range(1, FAR + 1):
            last = step == FAR
            up.append(moved(up[-1][:half_rows] if last else up[-1], ys, 1))
            down.append(moved(down[-1][half_rows:] if last else down[-1], ys, -1))
        ups.append(up)
        downs.append(down)

    res_t = residual.T
    gain_full = gain
    for position in range(y_bits):
        high = (dev_index >> position) % 2 == 1
        other_res = swapped(res_t, position)
        other_gain = swapped(gain_full, position)
        res_t = jnp.where(
            high,
            jnp.concatenate([other_res, res_t], 1),
            jnp.concatenate([res_t, other_res], 1),
        )
        gain_full = jnp.where(
            high,
            jnp.concatenate([other_gain, gain_full], 0),
            jnp.concatenate([gain_full, other_gain], 0),
        )
    gain_row = gain_full.astype(jnp.float32)[None, :]

    if columns % LANES:
        pick_of = lambda table_ref, distance: table_ref[distance]
    else:
        pick_of = lambda table_ref, distance: (
            slice(None),
            pl.ds(pl.multiple_of(table_ref[distance] * columns, LANES), columns),
        )
    weights = {}
    for far in ((4, 3, 5), (2, 6, 1), (7, 0)):
        blocks = regrouped(table, qkv_tile, far, (width, columns), pick_of)
        weights.update(zip(far, blocks))
    far_rows = regrouped(
        table,
        half_tiles,
        range(2),
        (half_rows, width),
        lambda table_ref, half: table_ref[FAR] * 2 + half,
    )

    near = FAR - 1
    acc = None
    for step in range(near):
        sides = [([up[step] for up in ups], -step), ([down[step] for down in downs], step)]
        acc = down_step(table, acc, 0, sides if step else sides[:1], chunk_tiles)
    sums = []
    for g, (low, high) in enumerate(bounds):
        sides = [([ups[g][near]], -near), ([downs[g][near]], near)]
        part = down_step(table, acc, low, sides, chunk_tiles)
        sums.append(last_step(part, [ups[g][FAR], downs[g][FAR]], far_rows, jnp.bfloat16))

    carry = columns >= max(high - low for low, high in bounds)
    blocks, parts = [], []
    for g, (low, high) in enumerate(bounds):
        mine = sums[g]
        for position in range(y_bits):
            theirs = swapped(mine, position)
            if position < y_bits - 1:
                mine = (mine.astype(jnp.float32) + theirs.astype(jnp.float32)).astype(jnp.bfloat16)
        block, scaled, squares, shard = finish(
            mine, theirs, res_t, low, gain_row, weights[FAR], columns, carry
        )
        blocks.append(block)
        far_way = 1 if g % 2 == 0 else -1
        came = []
        for by in (far_way, -far_way):
            held = None
            for distance in range(FAR if by == far_way else near, 0, -1):
                if distance == FAR:
                    held = shard
                else:
                    tile = weights[by * distance % XS]
                    held = hop(held, scaled, tile, squares, columns, carry)
                held = moved(held, ys, by)
            came.append(held)
        own_part = own_term(scaled, weights[0], columns)
        if not carry:
            for position in range(y_bits, y_bits + x_bits):
                squares = squares + swapped(squares, position)
        parts.append((own_part, squares, *came))
    stream = own_rows(low_index, blocks, own_width)
    qkv = last_sum(parts, carry)
    return (stream, qkv)


def solution(mesh):
    placed = (
        P("gx", "groups"),
        P("gx", "groups"),
        P("gx", None, None),
        P("gx"),
        P("gx", None, None),
    )
    return jax.shard_map(
        on_device,
        mesh=mesh,
        in_specs=placed,
        out_specs=(P("gx", "groups"), P("gx", "groups")),
        check_vma=False,
    )
```

profile of v0, /device:TPU:0, one launch (start us, length us, event | category | flops | bytes accessed | tf_op | source)
XLA Modules:
  0.0 243.0 jit_solution(8643987766789647740)
XLA Ops:
  0.6 1.4 token_slice.2.refs_0_
  2.1 3.1 %collective-permute-start = (bf16[2496,256]{1,0:T(8,128)(2,1)S(1)}, bf16[2496,256]{1,0:T(8,128)(2,1)S(1)}, u32[]{:S(2)}, u32[]{:S(2)}) collective-permute-start(bf16[2496,256]{1,0:T(8,128)(2,1)S(1)} %token_slice.2.refs_0_), channel_id=1, source_target_pairs={{0,4},{1,5},{4,8},{5,9},{8,12},{9,13},{12,14},{13,15},{14,10},{15,... | collective-permute-start | bytes 3833864 | tf_op jit(solution)/shard_map/ppermute | solution.py:39
  5.2 28.0 %collective-permute-done.refs_0_ = bf16[2496,256]{1,0:T(8,128)(2,1)S(1)} collective-permute-done((bf16[2496,256]{1,0:T(8,128)(2,1)S(1)}, bf16[2496,256]{1,0:T(8,128)(2,1)S(1)}, u32[]{:S(2)}, u32[]{:S(2)}) %collective-permute-start) | collective-permute-done | bytes 1277984 | tf_op jit(solution)/shard_map/ppermute | solution.py:39
  33.2 1.8 collective-permute-start.1
  35.2 1.5 token_slice.3.refs_1_
  36.7 1.6 collective-permute-start.8
  38.8 37.5 %collective-permute-done.8.refs_1_ = bf16[2496,128]{1,0:T(8,128)(2,1)} collective-permute-done((bf16[2496,128]{1,0:T(8,128)(2,1)S(1)}, bf16[2496,128]{1,0:T(8,128)(2,1)}, u32[]{:S(2)}, u32[]{:S(2)}) %collective-permute-start.8) | collective-permute-done | bytes 639008 | tf_op jit(solution)/shard_map/ppermute | solution.py:39
  76.2 1.5 collective-permute-start.9
  78.3 1.6 collective-permute-start.2
  80.4 2.3 copy.7
  82.7 8.2 %regrouped.4 = (bf16[1248,2048]{1,0:T(8,128)(2,1)}, bf16[1248,2048]{1,0:T(8,128)(2,1)}) custom-call(s32[8]{0:T(128)S(1)} %compare_select_fusion.2.table_ref, bf16[16,1248,2048]{2,1,0:T(8,128)(2,1)} %bitcast.1.source_ref), custom_call_target="tpu_custom_call" | custom-call | bytes 20447232 | tf_op jit(solution)/shard_map/regrouped/pallas_call | solution.py:206
  90.9 8.6 %down_step.5.refs_6_ = f32[384,2048]{1,0:T(8,128)S(1)} custom-call(s32[8]{0:T(128)S(1)} %compare_select_fusion.2.table_ref, bf16[2496,256]{1,0:T(8,128)(2,1)S(1)} %token_slice.2.refs_0_, bf16[2496,128]{1,0:T(8,128)(2,1)S(1)} %token_slice.3.refs_1_, bf16[8,2496,2048]{2,1,0:T(8,128)(2,1)} %bitcast.2.refs_2_.refs_4_.refs_5_.refs_3_), custom_call_target="tpu_custom_call" | custom-call | flops 3925868544 | bytes 18432000 | tf_op jit(solution)/shard_map/down_step/pallas_call | solution.py:92
  99.5 1.6 collective-permute-start.15
  101.6 13.9 %down_step.6.refs_6_ = f32[384,2048]{1,0:T(8,128)S(1)} custom-call(s32[8]{0:T(128)S(1)} %compare_select_fusion.2.table_ref, bf16[2496,256]{1,0:T(8,128)(2,1)S(1)} %copy-done.13, bf16[2496,128]{1,0:T(8,128)(2,1)} %collective-permute-done.8.refs_1_, bf16[2496,256]{1,0:T(8,128)(2,1)S(1)} %copy-done.15, bf16[2496,128]{1,0:T(8,128)(2,1)} %collective-permute-done.10.refs_3_, ...), custom_call_target="tpu_custom_call" | custom-call | flops 7851737088 | bytes 30572544 | tf_op jit(solution)/shard_map/down_step/pallas_call | solution.py:92
  115.5 5.6 %collective-permute-done.2.refs_0_ = bf16[2496,256]{1,0:T(8,128)(2,1)S(1)} collective-permute-done((bf16[2496,256]{1,0:T(8,128)(2,1)}, bf16[2496,256]{1,0:T(8,128)(2,1)S(1)}, u32[]{:S(2)}, u32[]{:S(2)}) %collective-permute-start.2) | collective-permute-done | bytes 1277984 | tf_op jit(solution)/shard_map/ppermute | solution.py:39
  121.1 1.6 collective-permute-start.3
  122.7 1.3 slice.17
  124.0 0.6 collective-permute-start.7
  124.6 15.1 %down_step.7.refs_4_ = f32[384,2048]{1,0:T(8,128)S(1)} custom-call(s32[8]{0:T(128)S(1)} %compare_select_fusion.2.table_ref, bf16[2496,256]{1,0:T(8,128)(2,1)} %collective-permute-done.1.refs_0_, bf16[2496,128]{1,0:T(8,128)(2,1)} %collective-permute-done.9.refs_1_, bf16[2496,256]{1,0:T(8,128)(2,1)} %collective-permute-done.5.refs_2_, ...), custom_call_target="tpu_custom_call" | custom-call | flops 7851737088 | bytes 30572544 | tf_op jit(solution)/shard_map/down_step/pallas_call | solution.py:92
  139.8 11.6 %down_step.8.refs_4_ = f32[256,2048]{1,0:T(8,128)S(1)} custom-call(s32[8]{0:T(128)S(1)} %compare_select_fusion.2.table_ref, bf16[2496,256]{1,0:T(8,128)(2,1)S(1)} %copy-done.11, bf16[2496,256]{1,0:T(8,128)(2,1)} %collective-permute-done.6.refs_1_, bf16[8,2496,2048]{2,1,0:T(8,128)(2,1)} %bitcast.2.refs_2_.refs_4_.refs_5_.refs_3_, ...), custom_call_target="tpu_custom_call" | custom-call | flops 5234491392 | bytes 27197440 | tf_op jit(solution)/shard_map/down_step/pallas_call | solution.py:92
  151.5 3.9 %shard_map.68.a = bf16[256,2048]{1,0:T(8,128)(2,1)} custom-call(bf16[1248,256]{1,0:T(8,128)(2,1)S(1)} %collective-permute-done.3.refs_0_, bf16[1248,256]{1,0:T(8,128)(2,1)S(1)} %collective-permute-done.7.refs_1_, bf16[1248,2048]{1,0:T(8,128)(2,1)S(1)} %bitcast.6, bf16[1248,2048]{1,0:T(8,128)(2,1)S(1)} %bitcast.10, f32[256,2048]{1,0:T(8,128)S(1)} %down_step.8.refs_4_), custom_call_target="tpu_custom_call" | custom-call | flops 2617245696 | bytes 13598720 | tf_op jit(solution)/shard_map/pallas_call | solution.py:225
  155.9 7.6 %regrouped.5 = (bf16[2048,640]{1,0:T(8,128)(2,1)}, bf16[2048,640]{1,0:T(8,128)(2,1)}, bf16[2048,640]{1,0:T(8,128)(2,1)}) custom-call(s32[8]{0:T(128)S(1)} %compare_select_fusion.2.table_ref, bf16[2048,5120]{1,0:T(8,128)(2,1)} %bitcast.13), custom_call_target="tpu_custom_call" | custom-call | bytes 15728640 | tf_op jit(solution)/shard_map/regrouped/pallas_call | solution.py:206
  163.6 1.0 slice.18
  164.6 1.6 collective-permute-start.16
  166.2 1.0 slice.19
  167.2 0.7 collective-permute-start.18
  167.9 2.1 maximum_select_fusion.r
  170.1 10.6 %down_step.9.refs_4_ = f32[128,2048]{1,0:T(8,128)S(1)} custom-call(s32[8]{0:T(128)S(1)} %compare_select_fusion.2.table_ref, bf16[2496,128]{1,0:T(8,128)(2,1)} %collective-permute-done.15.refs_0_, bf16[2496,128]{1,0:T(8,128)(2,1)} %collective-permute-done.17.refs_1_, bf16[8,2496,2048]{2,1,0:T(8,128)(2,1)} %bitcast.2.refs_2_.refs_4_.refs_5_.refs_3_, ...), custom_call_target="tpu_custom_call" | custom-call | flops 2617245696 | bytes 23822336 | tf_op jit(solution)/shard_map/down_step/pallas_call | solution.py:92
  180.7 3.8 %shard_map.69 = (bf16[256,2048]{1,0:T(8,128)(2,1)S(1)}, bf16[256,2048]{1,0:T(8,128)(2,1)S(1)}, f32[8,256]{1,0:T(8,128)S(1)}, bf16[264,640]{1,0:T(8,128)(2,1)S(1)}) custom-call(bf16[256,2048]{1,0:T(8,128)(2,1)} %shard_map.68.a, bf16[256,2048]{1,0:T(8,128)(2,1)} %collective-permute-done.12.b, bf16[384,2048]{1,0:T(8,128)(2,1)S(1)} %maximum_select_fusion.r, ...), custom_call_target="tpu_custom_call" | custom-call | flops 671088640 | bytes 6299648 | tf_op jit(solution)/shard_map/pallas_call | solution.py:225
  184.5 1.6 collective-permute-start.20
  186.2 1.6 shard_map.70.a
  187.9 1.0 shard_map.77
  188.9 0.5 collective-permute-start.24
  189.4 4.5 %collective-permute-done.20.refs_0_ = bf16[264,640]{1,0:T(8,128)(2,1)S(1)} collective-permute-done((bf16[264,640]{1,0:T(8,128)(2,1)S(1)}, bf16[264,640]{1,0:T(8,128)(2,1)S(1)}, u32[]{:S(2)}, u32[]{:S(2)}) %collective-permute-start.20) | collective-permute-done | bytes 337952 | tf_op jit(solution)/shard_map/ppermute | solution.py:39
  193.9 1.0 shard_map.74
  194.9 1.6 collective-permute-start.21
  196.5 1.2 shard_map.71
  198.2 7.7 %regrouped.7 = (bf16[2048,640]{1,0:T(8,128)(2,1)}, bf16[2048,640]{1,0:T(8,128)(2,1)}, bf16[2048,640]{1,0:T(8,128)(2,1)}) custom-call(s32[8]{0:T(128)S(1)} %compare_select_fusion.2.table_ref, bf16[2048,5120]{1,0:T(8,128)(2,1)} %bitcast.14), custom_call_target="tpu_custom_call" | custom-call | bytes 15728640 | tf_op jit(solution)/shard_map/regrouped/pallas_call | solution.py:206
  205.9 1.7 copy-done.7
  207.7 1.0 shard_map.78
  208.7 1.1 collective-permute-start.25
  209.8 1.0 shard_map.75
  210.8 1.2 collective-permute-start.22
  212.0 0.6 shard_map.84
  212.6 1.6 collective-permute-start.31
  214.2 0.6 shard_map.81
  215.3 4.6 %regrouped.6 = (bf16[2048,640]{1,0:T(8,128)(2,1)}, bf16[2048,640]{1,0:T(8,128)(2,1)}) custom-call(s32[8]{0:T(128)S(1)} %compare_select_fusion.2.table_ref, bf16[2048,5120]{1,0:T(8,128)(2,1)} %bitcast.15), custom_call_target="tpu_custom_call" | custom-call | bytes 10485760 | tf_op jit(solution)/shard_map/regrouped/pallas_call | solution.py:206
  219.9 2.3 collective-permute-done.31.refs_0_
  222.2 0.6 shard_map.85
  222.8 1.5 collective-permute-start.32
  224.3 0.6 shard_map.82
  224.9 0.7 collective-permute-start.29
  225.6 1.7 shard_map.79
  227.3 1.5 collective-permute-start.26
  228.8 1.7 shard_map.76
  231.1 1.3 shard_map.86
  232.3 1.4 collective-permute-start.33
  233.7 1.3 shard_map.83
  235.0 0.6 collective-permute-start.30
  235.6 1.7 copy-done.4
  237.4 0.6 shard_map.80.refs_4_
  238.0 1.1 shard_map.72
  239.1 1.0 shard_map.73.refs_0_
  240.7 2.2 shard_map.87
  (101 shorter events, 5.3 us)
Async XLA Ops:
  2.1 31.1 %collective-permute-start = (bf16[2496,256]{1,0:T(8,128)(2,1)S(1)}, bf16[2496,256]{1,0:T(8,128)(2,1)S(1)}, u32[]{:S(2)}, u32[]{:S(2)}) collective-permute-start(bf16[2496,256]{1,0:T(8,128)(2,1)S(1)} %token_slice.2.refs_0_), channel_id=1, source_target_pairs={{0,4},{1,5},{4,8},{5,9},{8,12},{9,13},{12,14},{13,15},{14,10},{15,... | collective-permute-start | bytes 3833864 | tf_op jit(solution)/shard_map/ppermute | solution.py:39
  5.2 29.8 %collective-permute-start.4 = (bf16[2496,256]{1,0:T(8,128)(2,1)S(1)}, bf16[2496,256]{1,0:T(8,128)(2,1)S(1)}, u32[]{:S(2)}, u32[]{:S(2)}) collective-permute-start(bf16[2496,256]{1,0:T(8,128)(2,1)S(1)} %token_slice.2.refs_0_), channel_id=1, source_target_pairs={{0,2},{1,3},{4,0},{5,1},{8,4},{9,5},{12,8},{13,9},{14,12},{15,13},... | collective-permute-start | bytes 3833864 | tf_op jit(solution)/shard_map/ppermute | solution.py:39
  33.2 45.1 %copy-start.12 = (bf16[2496,256]{1,0:T(8,128)(2,1)}, bf16[2496,256]{1,0:T(8,128)(2,1)S(1)}, u32[]{:S(2)}) copy-start(bf16[2496,256]{1,0:T(8,128)(2,1)S(1)} %collective-permute-done.refs_0_) | copy-start | bytes 3833860
  33.2 45.1 %collective-permute-start.1 = (bf16[2496,256]{1,0:T(8,128)(2,1)S(1)}, bf16[2496,256]{1,0:T(8,128)(2,1)}, u32[]{:S(2)}, u32[]{:S(2)}) collective-permute-start(bf16[2496,256]{1,0:T(8,128)(2,1)S(1)} %collective-permute-done.refs_0_), channel_id=1, source_target_pairs={{0,4},{1,5},{4,8},{5,9},{8,12},{9,13},{12,14},{13,15},{14,10},{15,... | collective-permute-start | bytes 3833864 | tf_op jit(solution)/shard_map/ppermute | solution.py:39
  35.0 43.3 %copy-start.14 = (bf16[2496,256]{1,0:T(8,128)(2,1)}, bf16[2496,256]{1,0:T(8,128)(2,1)S(1)}, u32[]{:S(2)}) copy-start(bf16[2496,256]{1,0:T(8,128)(2,1)S(1)} %collective-permute-done.4.refs_2_) | copy-start | bytes 3833860
  35.0 44.8 %collective-permute-start.5 = (bf16[2496,256]{1,0:T(8,128)(2,1)S(1)}, bf16[2496,256]{1,0:T(8,128)(2,1)}, u32[]{:S(2)}, u32[]{:S(2)}) collective-permute-start(bf16[2496,256]{1,0:T(8,128)(2,1)S(1)} %collective-permute-done.4.refs_2_), channel_id=1, source_target_pairs={{0,2},{1,3},{4,0},{5,1},{8,4},{9,5},{12,8},{13,9},{14,12},{15,13},... | collective-permute-start | bytes 3833864 | tf_op jit(solution)/shard_map/ppermute | solution.py:39
  36.7 39.5 %collective-permute-start.8 = (bf16[2496,128]{1,0:T(8,128)(2,1)S(1)}, bf16[2496,128]{1,0:T(8,128)(2,1)}, u32[]{:S(2)}, u32[]{:S(2)}) collective-permute-start(bf16[2496,128]{1,0:T(8,128)(2,1)S(1)} %token_slice.3.refs_1_), channel_id=1, source_target_pairs={{0,4},{1,5},{4,8},{5,9},{8,12},{9,13},{12,14},{13,15},{14,10},{15,... | collective-permute-start | bytes 1916936 | tf_op jit(solution)/shard_map/ppermute | solution.py:39
  38.3 39.4 %collective-permute-start.10 = (bf16[2496,128]{1,0:T(8,128)(2,1)S(1)}, bf16[2496,128]{1,0:T(8,128)(2,1)}, u32[]{:S(2)}, u32[]{:S(2)}) collective-permute-start(bf16[2496,128]{1,0:T(8,128)(2,1)S(1)} %token_slice.3.refs_1_), channel_id=1, source_target_pairs={{0,2},{1,3},{4,0},{5,1},{8,4},{9,5},{12,8},{13,9},{14,12},{15,13},... | collective-permute-start | bytes 1916936 | tf_op jit(solution)/shard_map/ppermute | solution.py:39
  76.2 23.2 %collective-permute-start.9 = (bf16[2496,128]{1,0:T(8,128)(2,1)}, bf16[2496,128]{1,0:T(8,128)(2,1)}, u32[]{:S(2)}, u32[]{:S(2)}) collective-permute-start(bf16[2496,128]{1,0:T(8,128)(2,1)} %collective-permute-done.8.refs_1_), channel_id=1, source_target_pairs={{0,4},{1,5},{4,8},{5,9},{8,12},{9,13},{12,14},{13,15},{14,10},{15,... | collective-permute-start | bytes 1916936 | tf_op jit(solution)/shard_map/ppermute | solution.py:39
  77.8 23.3 %collective-permute-start.11 = (bf16[2496,128]{1,0:T(8,128)(2,1)}, bf16[2496,128]{1,0:T(8,128)(2,1)}, u32[]{:S(2)}, u32[]{:S(2)}) collective-permute-start(bf16[2496,128]{1,0:T(8,128)(2,1)} %collective-permute-done.10.refs_3_), channel_id=1, source_target_pairs={{0,2},{1,3},{4,0},{5,1},{8,4},{9,5},{12,8},{13,9},{14,12},{15,13},... | collective-permute-start | bytes 1916936 | tf_op jit(solution)/shard_map/ppermute | solution.py:39
  78.3 42.8 %collective-permute-start.2 = (bf16[2496,256]{1,0:T(8,128)(2,1)}, bf16[2496,256]{1,0:T(8,128)(2,1)S(1)}, u32[]{:S(2)}, u32[]{:S(2)}) collective-permute-start(bf16[2496,256]{1,0:T(8,128)(2,1)} %collective-permute-done.1.refs_0_), channel_id=1, source_target_pairs={{0,4},{1,5},{4,8},{5,9},{8,12},{9,13},{12,14},{13,15},{14,10},{15,... | collective-permute-start | bytes 3833864 | tf_op jit(solution)/shard_map/ppermute | solution.py:39
  79.9 42.9 %collective-permute-start.6 = (bf16[2496,256]{1,0:T(8,128)(2,1)}, bf16[2496,256]{1,0:T(8,128)(2,1)}, u32[]{:S(2)}, u32[]{:S(2)}) collective-permute-start(bf16[2496,256]{1,0:T(8,128)(2,1)} %collective-permute-done.5.refs_2_), channel_id=1, source_target_pairs={{0,2},{1,3},{4,0},{5,1},{8,4},{9,5},{12,8},{13,9},{14,12},{15,13},... | collective-permute-start | bytes 3833864 | tf_op jit(solution)/shard_map/ppermute | solution.py:39
  82.7 85.3 %collective-permute-start.13 = (bf16[384,1024]{1,0:T(8,128)(2,1)}, bf16[384,1024]{1,0:T(8,128)(2,1)}, u32[]{:S(2)}, u32[]{:S(2)}) collective-permute-start(bf16[384,1024]{1,0:T(8,128)(2,1)} %bitcast.16), channel_id=1, source_target_pairs={{0,1},{1,0},{2,3},{3,2},{4,5},{5,4},{6,7},{7,6},{8,9},{9,8},{10,11... | collective-permute-start | bytes 2359304 | tf_op jit(solution)/shard_map/ppermute | solution.py:44
  90.9 10.7 %copy-start.13 = (bf16[2496,256]{1,0:T(8,128)(2,1)S(1)}, bf16[2496,256]{1,0:T(8,128)(2,1)}, u32[]{:S(2)}) copy-start(bf16[2496,256]{1,0:T(8,128)(2,1)} %copy-done.12) | copy-start | bytes 3833860
  90.9 10.7 %copy-start.15 = (bf16[2496,256]{1,0:T(8,128)(2,1)S(1)}, bf16[2496,256]{1,0:T(8,128)(2,1)}, u32[]{:S(2)}) copy-start(bf16[2496,256]{1,0:T(8,128)(2,1)} %copy-done.14) | copy-start | bytes 3833860
  99.5 64.1 %collective-permute-start.15 = (bf16[2496,128]{1,0:T(8,128)(2,1)}, bf16[2496,128]{1,0:T(8,128)(2,1)}, u32[]{:S(2)}, u32[]{:S(2)}) collective-permute-start(bf16[2496,128]{1,0:T(8,128)(2,1)} %collective-permute-done.9.refs_1_), channel_id=1, source_target_pairs={{0,4},{1,5},{4,8},{5,9},{8,12},{9,13},{12,14},{13,15},{14,10},{15,... | collective-permute-start | bytes 1916936 | tf_op jit(solution)/shard_map/ppermute | solution.py:39
  101.1 65.1 %collective-permute-start.17 = (bf16[2496,128]{1,0:T(8,128)(2,1)}, bf16[2496,128]{1,0:T(8,128)(2,1)}, u32[]{:S(2)}, u32[]{:S(2)}) collective-permute-start(bf16[2496,128]{1,0:T(8,128)(2,1)} %collective-permute-done.11.refs_3_), channel_id=1, source_target_pairs={{0,2},{1,3},{4,0},{5,1},{8,4},{9,5},{12,8},{13,9},{14,12},{15,13},... | collective-permute-start | bytes 1916936 | tf_op jit(solution)/shard_map/ppermute | solution.py:39
  121.1 2.9 %copy-start.10 = (bf16[2496,256]{1,0:T(8,128)(2,1)}, bf16[2496,256]{1,0:T(8,128)(2,1)S(1)}, u32[]{:S(2)}) copy-start(bf16[2496,256]{1,0:T(8,128)(2,1)S(1)} %collective-permute-done.2.refs_0_) | copy-start | bytes 3833860
  121.1 30.3 %collective-permute-start.3 = (bf16[1248,256]{1,0:T(8,128)(2,1)S(1)}, bf16[1248,256]{1,0:T(8,128)(2,1)S(1)}, u32[]{:S(2)}, u32[]{:S(2)}) collective-permute-start(bf16[1248,256]{1,0:T(8,128)(2,1)S(1)} %slice.16), channel_id=1, source_target_pairs={{0,4},{1,5},{4,8},{5,9},{8,12},{9,13},{12,14},{13,15},{14,10},{15,... | collective-permute-start | bytes 1916936 | tf_op jit(solution)/shard_map/ppermute | solution.py:39
  122.7 28.7 %slice-start = ((s8[5111808]{0:T(1024)(128)(4,1)}), s8[4194304]{0:T(1024)(128)(4,1)S(1)}, s32[]{:S(2)}) async-start(s8[5111808]{0:T(1024)(128)(4,1)} %bitcast.5), calls=%async_computation | async-start | bytes 8388608
  122.7 28.7 %slice-start.4 = ((s8[5111808]{0:T(1024)(128)(4,1)}), s8[4194304]{0:T(1024)(128)(4,1)S(1)}, s32[]{:S(2)}) async-start(s8[5111808]{0:T(1024)(128)(4,1)} %bitcast.9), calls=%async_computation.4 | async-start | bytes 8388608
  124.0 27.4 %slice-start.1 = ((s8[5111808]{0:T(1024)(128)(4,1)}), s8[917504]{0:T(1024)(128)(4,1)S(1)}, s32[]{:S(2)}) async-start(s8[5111808]{0:T(1024)(128)(4,1)} %bitcast.5), calls=%async_computation.1 | async-start | bytes 1835008
  124.0 27.4 %slice-start.5 = ((s8[5111808]{0:T(1024)(128)(4,1)}), s8[917504]{0:T(1024)(128)(4,1)S(1)}, s32[]{:S(2)}) async-start(s8[5111808]{0:T(1024)(128)(4,1)} %bitcast.9), calls=%async_computation.5 | async-start | bytes 1835008
  124.0 27.4 %collective-permute-start.7 = (bf16[1248,256]{1,0:T(8,128)(2,1)S(1)}, bf16[1248,256]{1,0:T(8,128)(2,1)S(1)}, u32[]{:S(2)}, u32[]{:S(2)}) collective-permute-start(bf16[1248,256]{1,0:T(8,128)(2,1)S(1)} %slice.17), channel_id=1, source_target_pairs={{0,2},{1,3},{4,0},{5,1},{8,4},{9,5},{12,8},{13,9},{14,12},{15,13},... | collective-permute-start | bytes 1916936 | tf_op jit(solution)/shard_map/ppermute | solution.py:39
  124.6 15.2 %copy-start.11 = (bf16[2496,256]{1,0:T(8,128)(2,1)S(1)}, bf16[2496,256]{1,0:T(8,128)(2,1)}, u32[]{:S(2)}) copy-start(bf16[2496,256]{1,0:T(8,128)(2,1)} %copy-done.10) | copy-start | bytes 3833860
  151.5 3.9 %copy-start.17 = (bf16[1024]{0:T(1024)(128)(2,1)S(1)}, bf16[1024]{0:T(1024)(128)(2,1)}, u32[]{:S(2)}) copy-start(bf16[1024]{0:T(1024)(128)(2,1)} %param.8) | copy-start | bytes 6148
  155.4 25.3 %collective-permute-start.12 = (bf16[256,2048]{1,0:T(8,128)(2,1)}, bf16[256,2048]{1,0:T(8,128)(2,1)}, u32[]{:S(2)}, u32[]{:S(2)}) collective-permute-start(bf16[256,2048]{1,0:T(8,128)(2,1)} %shard_map.68.a), channel_id=1, source_target_pairs={{0,1},{1,0},{2,3},{3,2},{4,5},{5,4},{6,7},{7,6},{8,9},{9,8},{10,11... | collective-permute-start | bytes 3145736 | tf_op jit(solution)/shard_map/ppermute | solution.py:44
  155.4 8.2 %collective-permute-start.14 = (bf16[1024]{0:T(1024)(128)(2,1)S(1)}, bf16[1024]{0:T(1024)(128)(2,1)S(1)}, u32[]{:S(2)}, u32[]{:S(2)}) collective-permute-start(bf16[1024]{0:T(1024)(128)(2,1)S(1)} %copy-done.17), channel_id=1, source_target_pairs={{0,1},{1,0},{2,3},{3,2},{4,5},{5,4},{6,7},{7,6},{8,9},{9,8},{10,11... | collective-permute-start | bytes 6152 | tf_op jit(solution)/shard_map/ppermute | solution.py:44
  155.9 12.0 %copy-start.16 = (bf16[1024,384]{0,1:T(8,128)(2,1)S(1)}, bf16[1024,384]{0,1:T(8,128)(2,1)}, u32[]{:S(2)}) copy-start(bf16[1024,384]{0,1:T(8,128)(2,1)} %copy.7) | copy-start | bytes 2359300
  164.6 21.5 %collective-permute-start.16 = (bf16[1248,128]{1,0:T(8,128)(2,1)S(1)}, bf16[1248,128]{1,0:T(8,128)(2,1)S(1)}, u32[]{:S(2)}, u32[]{:S(2)}) collective-permute-start(bf16[1248,128]{1,0:T(8,128)(2,1)S(1)} %slice.18), channel_id=1, source_target_pairs={{0,4},{1,5},{4,8},{5,9},{8,12},{9,13},{12,14},{13,15},{14,10},{15,... | collective-permute-start | bytes 958472 | tf_op jit(solution)/shard_map/ppermute | solution.py:39
  167.2 18.9 %collective-permute-start.18 = (bf16[1248,128]{1,0:T(8,128)(2,1)S(1)}, bf16[1248,128]{1,0:T(8,128)(2,1)S(1)}, u32[]{:S(2)}, u32[]{:S(2)}) collective-permute-start(bf16[1248,128]{1,0:T(8,128)(2,1)S(1)} %slice.19), channel_id=1, source_target_pairs={{0,2},{1,3},{4,0},{5,1},{8,4},{9,5},{12,8},{13,9},{14,12},{15,13},... | collective-permute-start | bytes 958472 | tf_op jit(solution)/shard_map/ppermute | solution.py:39
  167.9 18.2 %slice-start.2 = ((s8[5111808]{0:T(1024)(128)(4,1)}), s8[917504]{0:T(1024)(128)(4,1)S(1)}, s32[]{:S(2)}) async-start(s8[5111808]{0:T(1024)(128)(4,1)} %bitcast.7), calls=%async_computation.2 | async-start | bytes 1835008
  167.9 18.2 %slice-start.6 = ((s8[5111808]{0:T(1024)(128)(4,1)}), s8[4194304]{0:T(1024)(128)(4,1)S(1)}, s32[]{:S(2)}) async-start(s8[5111808]{0:T(1024)(128)(4,1)} %bitcast.11), calls=%async_computation.6 | async-start | bytes 8388608
  170.1 10.7 %copy-start.2 = (bf16[2048,640]{1,0:T(8,128)(2,1)S(1)}, bf16[2048,640]{1,0:T(8,128)(2,1)}, u32[]{:S(2)}) copy-start(bf16[2048,640]{1,0:T(8,128)(2,1)} %get-tuple-element.22.w) | copy-start | bytes 7864324
  170.1 16.1 %slice-start.3 = ((s8[5111808]{0:T(1024)(128)(4,1)}), s8[4194304]{0:T(1024)(128)(4,1)S(1)}, s32[]{:S(2)}) async-start(s8[5111808]{0:T(1024)(128)(4,1)} %bitcast.7), calls=%async_computation.3 | async-start | bytes 8388608
  170.1 16.1 %slice-start.7 = ((s8[5111808]{0:T(1024)(128)(4,1)}), s8[917504]{0:T(1024)(128)(4,1)S(1)}, s32[]{:S(2)}) async-start(s8[5111808]{0:T(1024)(128)(4,1)} %bitcast.11), calls=%async_computation.7 | async-start | bytes 1835008
  184.5 3.3 %copy-start = (bf16[2048,640]{1,0:T(8,128)(2,1)S(1)}, bf16[2048,640]{1,0:T(8,128)(2,1)}, u32[]{:S(2)}) copy-start(bf16[2048,640]{1,0:T(8,128)(2,1)} %get-tuple-element.32.refs_1_.refs_2_) | copy-start | bytes 7864324
  184.5 9.4 %collective-permute-start.20 = (bf16[264,640]{1,0:T(8,128)(2,1)S(1)}, bf16[264,640]{1,0:T(8,128)(2,1)S(1)}, u32[]{:S(2)}, u32[]{:S(2)}) collective-permute-start(bf16[264,640]{1,0:T(8,128)(2,1)S(1)} %get-tuple-element.28), channel_id=1, source_target_pairs={{0,4},{1,5},{4,8},{5,9},{8,12},{9,13},{12,14},{13,15},{14,10},{15,... | collective-permute-start | bytes 1013768 | tf_op jit(solution)/shard_map/ppermute | solution.py:39
  187.8 6.1 %copy-start.1 = (bf16[2048,640]{1,0:T(8,128)(2,1)S(1)}, bf16[2048,640]{1,0:T(8,128)(2,1)}, u32[]{:S(2)}) copy-start(bf16[2048,640]{1,0:T(8,128)(2,1)} %get-tuple-element.29.refs_2_.refs_1_) | copy-start | bytes 7864324
  187.8 8.7 %collective-permute-start.19 = (bf16[128,2048]{1,0:T(8,128)(2,1)S(1)}, bf16[128,2048]{1,0:T(8,128)(2,1)S(1)}, u32[]{:S(2)}, u32[]{:S(2)}) collective-permute-start(bf16[128,2048]{1,0:T(8,128)(2,1)S(1)} %shard_map.70.a), channel_id=1, source_target_pairs={{0,1},{1,0},{2,3},{3,2},{4,5},{5,4},{6,7},{7,6},{8,9},{9,8},{10,11... | collective-permute-start | bytes 1572872 | tf_op jit(solution)/shard_map/ppermute | solution.py:44
  188.9 17.0 %collective-permute-start.24 = (bf16[264,640]{1,0:T(8,128)(2,1)S(1)}, bf16[264,640]{1,0:T(8,128)(2,1)S(1)}, u32[]{:S(2)}, u32[]{:S(2)}) collective-permute-start(bf16[264,640]{1,0:T(8,128)(2,1)S(1)} %shard_map.77), channel_id=1, source_target_pairs={{0,2},{1,3},{4,0},{5,1},{8,4},{9,5},{12,8},{13,9},{14,12},{15,13},... | collective-permute-start | bytes 1013768 | tf_op jit(solution)/shard_map/ppermute | solution.py:39
  194.9 14.9 %collective-permute-start.21 = (bf16[264,640]{1,0:T(8,128)(2,1)S(1)}, bf16[264,640]{1,0:T(8,128)(2,1)S(1)}, u32[]{:S(2)}, u32[]{:S(2)}) collective-permute-start(bf16[264,640]{1,0:T(8,128)(2,1)S(1)} %shard_map.74), channel_id=1, source_target_pairs={{0,4},{1,5},{4,8},{5,9},{8,12},{9,13},{12,14},{13,15},{14,10},{15,... | collective-permute-start | bytes 1013768 | tf_op jit(solution)/shard_map/ppermute | solution.py:39
  197.7 16.5 %collective-permute-start.27 = (bf16[136,640]{1,0:T(8,128)(2,1)S(1)}, bf16[136,640]{1,0:T(8,128)(2,1)S(1)}, u32[]{:S(2)}, u32[]{:S(2)}) collective-permute-start(bf16[136,640]{1,0:T(8,128)(2,1)S(1)} %get-tuple-element.37), channel_id=1, source_target_pairs={{0,2},{1,3},{4,0},{5,1},{8,4},{9,5},{12,8},{13,9},{14,12},{15,13},... | collective-permute-start | bytes 522248 | tf_op jit(solution)/shard_map/ppermute | solution.py:39
  205.9 1.7 copy-start.7
  207.7 2.2 copy-start.9
  208.7 16.9 %collective-permute-start.25 = (bf16[264,640]{1,0:T(8,128)(2,1)S(1)}, bf16[264,640]{1,0:T(8,128)(2,1)S(1)}, u32[]{:S(2)}, u32[]{:S(2)}) collective-permute-start(bf16[264,640]{1,0:T(8,128)(2,1)S(1)} %shard_map.78), channel_id=1, source_target_pairs={{0,2},{1,3},{4,0},{5,1},{8,4},{9,5},{12,8},{13,9},{14,12},{15,13},... | collective-permute-start | bytes 1013768 | tf_op jit(solution)/shard_map/ppermute | solution.py:39
  210.8 18.0 %collective-permute-start.22 = (bf16[264,640]{1,0:T(8,128)(2,1)S(1)}, bf16[264,640]{1,0:T(8,128)(2,1)S(1)}, u32[]{:S(2)}, u32[]{:S(2)}) collective-permute-start(bf16[264,640]{1,0:T(8,128)(2,1)S(1)} %shard_map.75), channel_id=1, source_target_pairs={{0,4},{1,5},{4,8},{5,9},{8,12},{9,13},{12,14},{13,15},{14,10},{15,... | collective-permute-start | bytes 1013768 | tf_op jit(solution)/shard_map/ppermute | solution.py:39
  212.6 9.6 %collective-permute-start.31 = (bf16[136,640]{1,0:T(8,128)(2,1)S(1)}, bf16[136,640]{1,0:T(8,128)(2,1)S(1)}, u32[]{:S(2)}, u32[]{:S(2)}) collective-permute-start(bf16[136,640]{1,0:T(8,128)(2,1)S(1)} %shard_map.84), channel_id=1, source_target_pairs={{0,4},{1,5},{4,8},{5,9},{8,12},{9,13},{12,14},{13,15},{14,10},{15,... | collective-permute-start | bytes 522248 | tf_op jit(solution)/shard_map/ppermute | solution.py:39
  214.8 9.5 %collective-permute-start.28 = (bf16[136,640]{1,0:T(8,128)(2,1)S(1)}, bf16[136,640]{1,0:T(8,128)(2,1)S(1)}, u32[]{:S(2)}, u32[]{:S(2)}) collective-permute-start(bf16[136,640]{1,0:T(8,128)(2,1)S(1)} %shard_map.81), channel_id=1, source_target_pairs={{0,2},{1,3},{4,0},{5,1},{8,4},{9,5},{12,8},{13,9},{14,12},{15,13},... | collective-permute-start | bytes 522248 | tf_op jit(solution)/shard_map/ppermute | solution.py:39
  219.9 4.3 %copy-start.8 = (bf16[2048,640]{1,0:T(8,128)(2,1)S(1)}, bf16[2048,640]{1,0:T(8,128)(2,1)}, u32[]{:S(2)}) copy-start(bf16[2048,640]{1,0:T(8,128)(2,1)} %get-tuple-element.33.refs_2_) | copy-start | bytes 7864324
  222.8 2.8 %copy-start.6 = (bf16[2048,640]{1,0:T(8,128)(2,1)S(1)}, bf16[2048,640]{1,0:T(8,128)(2,1)}, u32[]{:S(2)}) copy-start(bf16[2048,640]{1,0:T(8,128)(2,1)} %get-tuple-element.34.refs_2_) | copy-start | bytes 7864324
  222.8 8.3 %collective-permute-start.32 = (bf16[136,640]{1,0:T(8,128)(2,1)S(1)}, bf16[136,640]{1,0:T(8,128)(2,1)S(1)}, u32[]{:S(2)}, u32[]{:S(2)}) collective-permute-start(bf16[136,640]{1,0:T(8,128)(2,1)S(1)} %shard_map.85), channel_id=1, source_target_pairs={{0,4},{1,5},{4,8},{5,9},{8,12},{9,13},{12,14},{13,15},{14,10},{15,... | collective-permute-start | bytes 522248 | tf_op jit(solution)/shard_map/ppermute | solution.py:39
  224.9 3.9 %copy-start.3 = (bf16[2048,640]{1,0:T(8,128)(2,1)S(1)}, bf16[2048,640]{1,0:T(8,128)(2,1)}, u32[]{:S(2)}) copy-start(bf16[2048,640]{1,0:T(8,128)(2,1)} %get-tuple-element.31.refs_2_) | copy-start | bytes 7864324
  224.9 8.9 %collective-permute-start.29 = (bf16[136,640]{1,0:T(8,128)(2,1)S(1)}, bf16[136,640]{1,0:T(8,128)(2,1)S(1)}, u32[]{:S(2)}, u32[]{:S(2)}) collective-permute-start(bf16[136,640]{1,0:T(8,128)(2,1)S(1)} %shard_map.82), channel_id=1, source_target_pairs={{0,2},{1,3},{4,0},{5,1},{8,4},{9,5},{12,8},{13,9},{14,12},{15,13},... | collective-permute-start | bytes 522248 | tf_op jit(solution)/shard_map/ppermute | solution.py:39
  227.3 13.4 %collective-permute-start.26 = (bf16[264,640]{1,0:T(8,128)(2,1)}, bf16[264,640]{1,0:T(8,128)(2,1)S(1)}, u32[]{:S(2)}, u32[]{:S(2)}) collective-permute-start(bf16[264,640]{1,0:T(8,128)(2,1)} %shard_map.79), channel_id=1, source_target_pairs={{0,2},{1,3},{4,0},{5,1},{8,4},{9,5},{12,8},{13,9},{14,12},{15,13},... | collective-permute-start | bytes 1013768 | tf_op jit(solution)/shard_map/ppermute | solution.py:39
  230.5 10.2 %collective-permute-start.23 = (bf16[264,640]{1,0:T(8,128)(2,1)}, bf16[264,640]{1,0:T(8,128)(2,1)}, u32[]{:S(2)}, u32[]{:S(2)}) collective-permute-start(bf16[264,640]{1,0:T(8,128)(2,1)} %shard_map.76), channel_id=1, source_target_pairs={{0,4},{1,5},{4,8},{5,9},{8,12},{9,13},{12,14},{13,15},{14,10},{15,... | collective-permute-start | bytes 1013768 | tf_op jit(solution)/shard_map/ppermute | solution.py:39
  232.3 8.2 %collective-permute-start.33 = (bf16[136,640]{1,0:T(8,128)(2,1)}, bf16[136,640]{1,0:T(8,128)(2,1)}, u32[]{:S(2)}, u32[]{:S(2)}) collective-permute-start(bf16[136,640]{1,0:T(8,128)(2,1)} %shard_map.86), channel_id=1, source_target_pairs={{0,4},{1,5},{4,8},{5,9},{8,12},{9,13},{12,14},{13,15},{14,10},{15,... | collective-permute-start | bytes 522248 | tf_op jit(solution)/shard_map/ppermute | solution.py:39
  235.0 5.7 %collective-permute-start.30 = (bf16[136,640]{1,0:T(8,128)(2,1)}, bf16[136,640]{1,0:T(8,128)(2,1)}, u32[]{:S(2)}, u32[]{:S(2)}) collective-permute-start(bf16[136,640]{1,0:T(8,128)(2,1)} %shard_map.83), channel_id=1, source_target_pairs={{0,2},{1,3},{4,0},{5,1},{8,4},{9,5},{12,8},{13,9},{14,12},{15,13},... | collective-permute-start | bytes 522248 | tf_op jit(solution)/shard_map/ppermute | solution.py:39
  235.6 1.7 copy-start.4
  237.4 1.7 copy-start.5
where the time goes:
time: 244 us; the launch traced here: 243 us
  Pallas kernels  119 us (49%)
  waiting for transfers between devices  78.5 us (32%)
  starting transfers between devices  33.3 us (14%)
  local copies, waits for them, and re-layouts  9.17 us (4%)
    ppermute x30, waiting for transfers between devices, moved(): return lax.ppermute(value, 'gx', route)  78.5 us
    pallas_call x5, Pallas kernels, down_step(): pl.pallas_call(body, grid_spec=pltpu.PrefetchScalarGridSpec(num_scalar_pr...  59.8 us
    ppermute x30, starting transfers between devices, moved(): return lax.ppermute(value, 'gx', route)  32.7 us
    pallas_call x4, Pallas kernels, regrouped(): pl.pallas_call(body, in_specs=[IN_SMEM, in_hbm], out_specs=[in_hbm] * cou...  28.1 us
    pallas_call x20, Pallas kernels, small_call(): pl.pallas_call(body, in_specs=[IN_SMEM] * smem + [IN_VMEM] * (len(operand...  27.8 us
    unnamed x53, local copies, waits for them, and re-layouts  5.86 us
  transfers between devices with their start and end apart: 34, of which 7 were waited for; matrix products, arithmetic and copies ran while one was open for 3% of the time, Pallas kernels for 47%

commit v1 on v0

--- a/solution.py
+++ b/solution.py
@@ -53,6 +53,7 @@
 def down_step(table, acc, low, sides, tiles):
     count, groups = len(sides), len(sides[0][0])
     rows, width = tiles.shape[1:]
+    parts = tiles.shape[0] // XS
     widths = [piece.shape[1] for piece in sides[0][0]]
     size = sum(widths)
     block = min(width, 512)
@@ -78,13 +79,13 @@
     def piece_spec(tokens):
         return pl.BlockSpec((rows, tokens), lambda i, table: (0, 0), pipeline_mode=pl.Buffered(1))
 
-    def weight_spec(distance):
+    def weight_spec(distance, part):
         at = distance % XS
-        return pl.BlockSpec((1, rows, block), lambda i, table: (table[at], 0, i))
+        return pl.BlockSpec((1, rows, block), lambda i, table: (table[at] * parts + part, 0, i))
 
     in_specs = [piece_spec(tokens) for _ in sides for tokens in widths]
-    in_specs += [weight_spec(far) for _, far in sides]
-    operands = [piece for pieces, _ in sides for piece in pieces] + [tiles] * count
+    in_specs += [weight_spec(far, part) for _, far, part in sides]
+    operands = [piece for pieces, _, _ in sides for piece in pieces] + [tiles] * count
     if acc is not None:
         in_specs.append(pl.BlockSpec((size, block), lambda i, table: (low // size, i)))
         operands.append(acc)
@@ -386,14 +387,31 @@
 
     bounds = token_groups(tokens)
 
+    near = FAR - 1
+    split = len(bounds) > 1
     ups, downs = [], []
-    for low, high in bounds:
+    for g, (low, high) in enumerate(bounds):
         own = token_slice(hidden, low, high)
         up, down = [own], [own]
         for step in range(1, FAR + 1):
+            if step == near and split and g == 0:
+                parts = {}
+                for h in range(2):
+                    rows = slice(h * half_rows, (h + 1) * half_rows)
+                    parts["u", h] = moved(up[-1][rows], ys, 1)
+                    parts["d", h] = moved(down[-1][rows], ys, -1)
+                up.append((parts["u", 0], parts["u", 1]))
+                down.append((parts["d", 0], parts["d", 1]))
+                continue
             last = step == FAR
-            up.append(moved(up[-1][:half_rows] if last else up[-1], ys, 1))
-            down.append(moved(down[-1][half_rows:] if last else down[-1], ys, -1))
+            if last:
+                halves = isinstance(up[-1], tuple)
+                up_sent = up[-1][0] if halves else up[-1][:half_rows]
+                down_sent = down[-1][1] if halves else down[-1][half_rows:]
+            else:
+                up_sent, down_sent = up[-1], down[-1]
+            up.append(moved(up_sent, ys, 1))
+            down.append(moved(down_sent, ys, -1))
         ups.append(up)
         downs.append(down)
 
@@ -434,15 +452,22 @@
         lambda table_ref, half: table_ref[FAR] * 2 + half,
     )
 
-    near = FAR - 1
     acc = None
     for step in range(near):
-        sides = [([up[step] for up in ups], -step), ([down[step] for down in downs], step)]
+        sides = [([up[step] for up in ups], -step, 0), ([down[step] for down in downs], step, 0)]
         acc = down_step(table, acc, 0, sides if step else sides[:1], chunk_tiles)
     sums = []
     for g, (low, high) in enumerate(bounds):
-        sides = [([ups[g][near]], -near), ([downs[g][near]], near)]
-        part = down_step(table, acc, low, sides, chunk_tiles)
+        up, down = ups[g][near], downs[g][near]
+        if isinstance(up, tuple):
+            part, start = acc, low
+            for h in (0, 1):
+                sides = [([up[h]], -near, h), ([down[1 - h]], near, 1 - h)]
+                part = down_step(table, part, start, sides, half_tiles)
+                start = 0
+        else:
+            sides = [([up], -near, 0), ([down], near, 0)]
+            part = down_step(table, acc, low, sides, chunk_tiles)
         sums.append(last_step(part, [ups[g][FAR], downs[g][FAR]], far_rows, jnp.bfloat16))
 
     carry = columns >= max(high - low for low, high in bounds)

time: 244 us -> 235 us (0.963)
  waiting for transfers between devices: 78.5 us -> 63.6 us
  Pallas kernels: 119 us -> 122 us
    ppermute x30 -> x32, waiting for transfers between devices: 78.5 us -> 63.6 us  [moved(): return lax.ppermute(value, 'gx', route)]
    pallas_call x5 -> x6, Pallas kernels: 59.8 us -> 63 us  [down_step(): pl.pallas_call(body, grid_spec=pltpu.PrefetchScalarGridSpec(num_scalar_pr...]
    ppermute x30 -> x32, starting transfers between devices: 32.7 us -> 34.7 us  [moved(): return lax.ppermute(value, 'gx', route)]
    unnamed x53 -> x45, local copies, waits for them, and re-layouts: 5.86 us -> 7.14 us
  transfers between devices with their start and end apart: 34 -> 36, of which waited for: 7 -> 6; matrix products, arithmetic and copies ran while one was open for 3% -> 3% of each run, Pallas kernels for 47% -> 50%
where the time goes in v1:
time: 235 us; the launch traced here: 234 us
  Pallas kernels  122 us (52%)
  waiting for transfers between devices  63.6 us (27%)
  starting transfers between devices  35.3 us (15%)
  local copies, waits for them, and re-layouts  10.6 us (5%)
    ppermute x32, waiting for transfers between devices, moved(): return lax.ppermute(value, 'gx', route)  63.6 us
    pallas_call x6, Pallas kernels, down_step(): pl.pallas_call(body, grid_spec=pltpu.PrefetchScalarGridSpec(num_scalar_pr...  63 us
    ppermute x32, starting transfers between devices, moved(): return lax.ppermute(value, 'gx', route)  34.7 us
    pallas_call x4, Pallas kernels, regrouped(): pl.pallas_call(body, in_specs=[IN_SMEM, in_hbm], out_specs=[in_hbm] * cou...  28.1 us
    pallas_call x20, Pallas kernels, small_call(): pl.pallas_call(body, in_specs=[IN_SMEM] * smem + [IN_VMEM] * (len(operand...  27.9 us
    unnamed x45, local copies, waits for them, and re-layouts  7.14 us
  transfers between devices with their start and end apart: 36, of which 6 were waited for; matrix products, arithmetic and copies ran while one was open for 3% of the time, Pallas kernels for 50%

profile of v1, /device:TPU:0, one launch (start us, length us, event | category | flops | bytes accessed | tf_op | source)
XLA Modules:
  0.0 234.3 jit_solution(7332989222663271788)
XLA Ops:
  0.6 1.4 token_slice.2.refs_0_
  2.1 3.1 %collective-permute-start = (bf16[2496,256]{1,0:T(8,128)(2,1)S(1)}, bf16[2496,256]{1,0:T(8,128)(2,1)}, u32[]{:S(2)}, u32[]{:S(2)}) collective-permute-start(bf16[2496,256]{1,0:T(8,128)(2,1)S(1)} %token_slice.2.refs_0_), channel_id=1, source_target_pairs={{0,4},{1,5},{4,8},{5,9},{8,12},{9,13},{12,14},{13,15},{14,10},{15,... | collective-permute-start | bytes 3833864 | tf_op jit(solution)/shard_map/ppermute | solution.py:39
  5.2 28.1 %collective-permute-done.refs_0_ = bf16[2496,256]{1,0:T(8,128)(2,1)} collective-permute-done((bf16[2496,256]{1,0:T(8,128)(2,1)S(1)}, bf16[2496,256]{1,0:T(8,128)(2,1)}, u32[]{:S(2)}, u32[]{:S(2)}) %collective-permute-start) | collective-permute-done | bytes 1277984 | tf_op jit(solution)/shard_map/ppermute | solution.py:39
  33.3 1.8 collective-permute-start.1
  35.3 1.2 token_slice.3.refs_1_
  36.6 1.8 collective-permute-start.10
  38.7 2.3 copy.7
  41.0 8.2 %regrouped.4 = (bf16[1248,2048]{1,0:T(8,128)(2,1)}, bf16[1248,2048]{1,0:T(8,128)(2,1)}) custom-call(s32[8]{0:T(128)S(1)} %compare_select_fusion.2.table_ref, bf16[16,1248,2048]{2,1,0:T(8,128)(2,1)} %bitcast.1.source_ref.refs_2_.refs_3_), custom_call_target="tpu_custom_call" | custom-call | bytes 20447232 | tf_op jit(solution)/shard_map/regrouped/pallas_call | solution.py:207
  49.2 8.4 %down_step.6.refs_6_ = f32[384,2048]{1,0:T(8,128)S(1)} custom-call(s32[8]{0:T(128)S(1)} %compare_select_fusion.2.table_ref, bf16[2496,256]{1,0:T(8,128)(2,1)S(1)} %token_slice.2.refs_0_, bf16[2496,128]{1,0:T(8,128)(2,1)S(1)} %token_slice.3.refs_1_, bf16[8,2496,2048]{2,1,0:T(8,128)(2,1)} %bitcast.2.refs_2_.refs_4_.refs_5_.refs_3_), custom_call_target="tpu_custom_call" | custom-call | flops 3925868544 | bytes 18432000 | tf_op jit(solution)/shard_map/down_step/pallas_call | solution.py:93
  57.6 19.0 %collective-permute-done.10.refs_1_ = bf16[2496,128]{1,0:T(8,128)(2,1)} collective-permute-done((bf16[2496,128]{1,0:T(8,128)(2,1)S(1)}, bf16[2496,128]{1,0:T(8,128)(2,1)}, u32[]{:S(2)}, u32[]{:S(2)}) %collective-permute-start.10) | collective-permute-done | bytes 639008 | tf_op jit(solution)/shard_map/ppermute | solution.py:39
  76.6 1.5 collective-permute-start.11
  78.7 1.6 collective-permute-start.2
  80.3 1.4 fusion.2
  82.2 14.6 %down_step.7.refs_6_ = f32[384,2048]{1,0:T(8,128)S(1)} custom-call(s32[8]{0:T(128)S(1)} %compare_select_fusion.2.table_ref, bf16[2496,256]{1,0:T(8,128)(2,1)} %collective-permute-done.refs_0_, bf16[2496,128]{1,0:T(8,128)(2,1)} %collective-permute-done.10.refs_1_, bf16[2496,256]{1,0:T(8,128)(2,1)} %collective-permute-done.4.refs_2_, ...), custom_call_target="tpu_custom_call" | custom-call | flops 7851737088 | bytes 30572544 | tf_op jit(solution)/shard_map/down_step/pallas_call | solution.py:93
  96.8 1.6 collective-permute-start.8
  98.9 8.8 %collective-permute-done.2.refs_0_ = bf16[1248,256]{1,0:T(8,128)(2,1)S(1)} collective-permute-done((bf16[1248,256]{1,0:T(8,128)(2,1)S(1)}, bf16[1248,256]{1,0:T(8,128)(2,1)S(1)}, u32[]{:S(2)}, u32[]{:S(2)}) %collective-permute-start.2) | collective-permute-done | bytes 639008 | tf_op jit(solution)/shard_map/ppermute | solution.py:39
  107.7 1.5 collective-permute-start.3
  109.7 1.3 copy-done.11
  111.1 14.5 %down_step.8.refs_4_ = f32[384,2048]{1,0:T(8,128)S(1)} custom-call(s32[8]{0:T(128)S(1)} %compare_select_fusion.2.table_ref, bf16[2496,256]{1,0:T(8,128)(2,1)S(1)} %copy-done.11, bf16[2496,128]{1,0:T(8,128)(2,1)} %collective-permute-done.11.refs_1_, bf16[2496,256]{1,0:T(8,128)(2,1)} %collective-permute-done.5.refs_2_, ...), custom_call_target="tpu_custom_call" | custom-call | flops 7851737088 | bytes 30572544 | tf_op jit(solution)/shard_map/down_step/pallas_call | solution.py:93
  125.6 7.6 %down_step.9.refs_4_ = f32[256,2048]{1,0:T(8,128)S(1)} custom-call(s32[8]{0:T(128)S(1)} %compare_select_fusion.2.table_ref, bf16[1248,256]{1,0:T(8,128)(2,1)S(1)} %collective-permute-done.2.refs_0_, bf16[1248,256]{1,0:T(8,128)(2,1)S(1)} %collective-permute-done.6.refs_1_, bf16[16,1248,2048]{2,1,0:T(8,128)(2,1)} %bitcast.1.source_ref.refs_2_.refs_3_, ...), custom_call_target="tpu_custom_call" | custom-call | flops 2617245696 | bytes 15695872 | tf_op jit(solution)/shard_map/down_step/pallas_call | solution.py:93
  133.2 1.6 collective-permute-start.17
  135.3 7.3 %down_step.10.refs_4_ = f32[256,2048]{1,0:T(8,128)S(1)} custom-call(s32[8]{0:T(128)S(1)} %compare_select_fusion.2.table_ref, bf16[1248,256]{1,0:T(8,128)(2,1)S(1)} %collective-permute-done.8.refs_0_, bf16[1248,256]{1,0:T(8,128)(2,1)S(1)} %collective-permute-done.9.refs_1_, bf16[16,1248,2048]{2,1,0:T(8,128)(2,1)} %bitcast.1.source_ref.refs_2_.refs_3_, ...), custom_call_target="tpu_custom_call" | custom-call | flops 2617245696 | bytes 15695872 | tf_op jit(solution)/shard_map/down_step/pallas_call | solution.py:93
  142.7 3.9 %shard_map.68.a = bf16[256,2048]{1,0:T(8,128)(2,1)} custom-call(bf16[1248,256]{1,0:T(8,128)(2,1)S(1)} %collective-permute-done.3.refs_0_, bf16[1248,256]{1,0:T(8,128)(2,1)S(1)} %collective-permute-done.7.refs_1_, bf16[1248,2048]{1,0:T(8,128)(2,1)S(1)} %bitcast.6, bf16[1248,2048]{1,0:T(8,128)(2,1)S(1)} %bitcast.10, f32[256,2048]{1,0:T(8,128)S(1)} %down_step.10.refs_4_), custom_call_target="tpu_custom_call" | custom-call | flops 2617245696 | bytes 13598720 | tf_op jit(solution)/shard_map/pallas_call | solution.py:226
  147.1 7.6 %regrouped.5 = (bf16[2048,640]{1,0:T(8,128)(2,1)}, bf16[2048,640]{1,0:T(8,128)(2,1)}, bf16[2048,640]{1,0:T(8,128)(2,1)}) custom-call(s32[8]{0:T(128)S(1)} %compare_select_fusion.2.table_ref, bf16[2048,5120]{1,0:T(8,128)(2,1)} %bitcast.13), custom_call_target="tpu_custom_call" | custom-call | bytes 15728640 | tf_op jit(solution)/shard_map/regrouped/pallas_call | solution.py:207
  154.8 1.0 slice.28
  155.8 1.6 collective-permute-start.18
  157.4 1.0 slice.29
  158.4 0.7 collective-permute-start.20
  159.1 2.0 maximum_select_fusion.r
  161.1 10.6 %down_step.11.refs_4_ = f32[128,2048]{1,0:T(8,128)S(1)} custom-call(s32[8]{0:T(128)S(1)} %compare_select_fusion.2.table_ref, bf16[2496,128]{1,0:T(8,128)(2,1)} %collective-permute-done.17.refs_0_, bf16[2496,128]{1,0:T(8,128)(2,1)} %collective-permute-done.19.refs_1_, bf16[8,2496,2048]{2,1,0:T(8,128)(2,1)} %bitcast.2.refs_2_.refs_4_.refs_5_.refs_3_, ...), custom_call_target="tpu_custom_call" | custom-call | flops 2617245696 | bytes 23822336 | tf_op jit(solution)/shard_map/down_step/pallas_call | solution.py:93
  171.8 3.8 %shard_map.69 = (bf16[256,2048]{1,0:T(8,128)(2,1)S(1)}, bf16[256,2048]{1,0:T(8,128)(2,1)S(1)}, f32[8,256]{1,0:T(8,128)S(1)}, bf16[264,640]{1,0:T(8,128)(2,1)S(1)}) custom-call(bf16[256,2048]{1,0:T(8,128)(2,1)} %shard_map.68.a, bf16[256,2048]{1,0:T(8,128)(2,1)} %collective-permute-done.14.b, bf16[384,2048]{1,0:T(8,128)(2,1)S(1)} %maximum_select_fusion.r, ...), custom_call_target="tpu_custom_call" | custom-call | flops 671088640 | bytes 6299648 | tf_op jit(solution)/shard_map/pallas_call | solution.py:226
  175.6 1.6 collective-permute-start.22
  177.2 1.6 shard_map.70.a
  178.9 1.0 shard_map.77
  180.5 4.5 %collective-permute-done.22.refs_0_ = bf16[264,640]{1,0:T(8,128)(2,1)S(1)} collective-permute-done((bf16[264,640]{1,0:T(8,128)(2,1)S(1)}, bf16[264,640]{1,0:T(8,128)(2,1)S(1)}, u32[]{:S(2)}, u32[]{:S(2)}) %collective-permute-start.22) | collective-permute-done | bytes 337952 | tf_op jit(solution)/shard_map/ppermute | solution.py:39
  185.0 1.0 shard_map.74
  186.0 1.6 collective-permute-start.23
  187.6 1.2 shard_map.71
  189.3 7.7 %regrouped.7 = (bf16[2048,640]{1,0:T(8,128)(2,1)}, bf16[2048,640]{1,0:T(8,128)(2,1)}, bf16[2048,640]{1,0:T(8,128)(2,1)}) custom-call(s32[8]{0:T(128)S(1)} %compare_select_fusion.2.table_ref, bf16[2048,5120]{1,0:T(8,128)(2,1)} %bitcast.14), custom_call_target="tpu_custom_call" | custom-call | bytes 15728640 | tf_op jit(solution)/shard_map/regrouped/pallas_call | solution.py:207
  197.0 1.7 copy-done.7
  198.8 1.0 shard_map.78
  199.8 1.5 collective-permute-start.27
  201.3 1.0 shard_map.75
  202.3 0.8 collective-permute-start.24
  203.1 0.6 shard_map.84
  203.7 1.6 collective-permute-start.33
  205.3 0.6 shard_map.81
  206.4 4.6 %regrouped.6 = (bf16[2048,640]{1,0:T(8,128)(2,1)}, bf16[2048,640]{1,0:T(8,128)(2,1)}) custom-call(s32[8]{0:T(128)S(1)} %compare_select_fusion.2.table_ref, bf16[2048,5120]{1,0:T(8,128)(2,1)} %bitcast.15), custom_call_target="tpu_custom_call" | custom-call | bytes 10485760 | tf_op jit(solution)/shard_map/regrouped/pallas_call | solution.py:207
  211.0 2.7 %collective-permute-done.33.refs_0_ = bf16[136,640]{1,0:T(8,128)(2,1)S(1)} collective-permute-done((bf16[136,640]{1,0:T(8,128)(2,1)S(1)}, bf16[136,640]{1,0:T(8,128)(2,1)S(1)}, u32[]{:S(2)}, u32[]{:S(2)}) %collective-permute-start.33) | collective-permute-done | bytes 174112 | tf_op jit(solution)/shard_map/ppermute | solution.py:39
  213.7 0.6 shard_map.85
  214.3 1.1 collective-permute-start.34
  215.4 0.6 shard_map.82
  216.0 1.1 collective-permute-start.31
  217.0 1.7 shard_map.79
  218.8 1.6 collective-permute-start.28
  220.4 1.7 shard_map.76
  222.6 1.3 shard_map.86
  223.8 1.0 collective-permute-start.35
  224.8 1.3 shard_map.83
  226.1 1.0 collective-permute-start.32
  227.1 1.7 copy-done.4
  229.5 1.1 shard_map.72
  230.6 1.0 shard_map.73.refs_0_
  232.1 2.3 shard_map.87
  (98 shorter events, 7.0 us)
Async XLA Ops:
  2.1 31.2 %collective-permute-start = (bf16[2496,256]{1,0:T(8,128)(2,1)S(1)}, bf16[2496,256]{1,0:T(8,128)(2,1)}, u32[]{:S(2)}, u32[]{:S(2)}) collective-permute-start(bf16[2496,256]{1,0:T(8,128)(2,1)S(1)} %token_slice.2.refs_0_), channel_id=1, source_target_pairs={{0,4},{1,5},{4,8},{5,9},{8,12},{9,13},{12,14},{13,15},{14,10},{15,... | collective-permute-start | bytes 3833864 | tf_op jit(solution)/shard_map/ppermute | solution.py:39
  5.2 29.9 %collective-permute-start.4 = (bf16[2496,256]{1,0:T(8,128)(2,1)S(1)}, bf16[2496,256]{1,0:T(8,128)(2,1)}, u32[]{:S(2)}, u32[]{:S(2)}) collective-permute-start(bf16[2496,256]{1,0:T(8,128)(2,1)S(1)} %token_slice.2.refs_0_), channel_id=1, source_target_pairs={{0,2},{1,3},{4,0},{5,1},{8,4},{9,5},{12,8},{13,9},{14,12},{15,13},... | collective-permute-start | bytes 3833864 | tf_op jit(solution)/shard_map/ppermute | solution.py:39
  33.3 45.3 %collective-permute-start.1 = (bf16[2496,256]{1,0:T(8,128)(2,1)}, bf16[2496,256]{1,0:T(8,128)(2,1)S(1)}, u32[]{:S(2)}, u32[]{:S(2)}) collective-permute-start(bf16[2496,256]{1,0:T(8,128)(2,1)} %collective-permute-done.refs_0_), channel_id=1, source_target_pairs={{0,4},{1,5},{4,8},{5,9},{8,12},{9,13},{12,14},{13,15},{14,10},{15,... | collective-permute-start | bytes 3833864 | tf_op jit(solution)/shard_map/ppermute | solution.py:39
  35.1 45.1 %collective-permute-start.5 = (bf16[2496,256]{1,0:T(8,128)(2,1)}, bf16[2496,256]{1,0:T(8,128)(2,1)}, u32[]{:S(2)}, u32[]{:S(2)}) collective-permute-start(bf16[2496,256]{1,0:T(8,128)(2,1)} %collective-permute-done.4.refs_2_), channel_id=1, source_target_pairs={{0,2},{1,3},{4,0},{5,1},{8,4},{9,5},{12,8},{13,9},{14,12},{15,13},... | collective-permute-start | bytes 3833864 | tf_op jit(solution)/shard_map/ppermute | solution.py:39
  36.6 40.0 %collective-permute-start.10 = (bf16[2496,128]{1,0:T(8,128)(2,1)S(1)}, bf16[2496,128]{1,0:T(8,128)(2,1)}, u32[]{:S(2)}, u32[]{:S(2)}) collective-permute-start(bf16[2496,128]{1,0:T(8,128)(2,1)S(1)} %token_slice.3.refs_1_), channel_id=1, source_target_pairs={{0,4},{1,5},{4,8},{5,9},{8,12},{9,13},{12,14},{13,15},{14,10},{15,... | collective-permute-start | bytes 1916936 | tf_op jit(solution)/shard_map/ppermute | solution.py:39
  38.4 39.7 %collective-permute-start.12 = (bf16[2496,128]{1,0:T(8,128)(2,1)S(1)}, bf16[2496,128]{1,0:T(8,128)(2,1)}, u32[]{:S(2)}, u32[]{:S(2)}) collective-permute-start(bf16[2496,128]{1,0:T(8,128)(2,1)S(1)} %token_slice.3.refs_1_), channel_id=1, source_target_pairs={{0,2},{1,3},{4,0},{5,1},{8,4},{9,5},{12,8},{13,9},{14,12},{15,13},... | collective-permute-start | bytes 1916936 | tf_op jit(solution)/shard_map/ppermute | solution.py:39
  40.9 118.2 %collective-permute-start.15 = (bf16[384,1024]{1,0:T(8,128)(2,1)}, bf16[384,1024]{1,0:T(8,128)(2,1)}, u32[]{:S(2)}, u32[]{:S(2)}) collective-permute-start(bf16[384,1024]{1,0:T(8,128)(2,1)} %bitcast.16), channel_id=1, source_target_pairs={{0,1},{1,0},{2,3},{3,2},{4,5},{5,4},{6,7},{7,6},{8,9},{9,8},{10,11... | collective-permute-start | bytes 2359304 | tf_op jit(solution)/shard_map/ppermute | solution.py:44
  76.6 20.3 %collective-permute-start.11 = (bf16[2496,128]{1,0:T(8,128)(2,1)}, bf16[2496,128]{1,0:T(8,128)(2,1)}, u32[]{:S(2)}, u32[]{:S(2)}) collective-permute-start(bf16[2496,128]{1,0:T(8,128)(2,1)} %collective-permute-done.10.refs_1_), channel_id=1, source_target_pairs={{0,4},{1,5},{4,8},{5,9},{8,12},{9,13},{12,14},{13,15},{14,10},{15,... | collective-permute-start | bytes 1916936 | tf_op jit(solution)/shard_map/ppermute | solution.py:39
  78.1 20.4 %collective-permute-start.13 = (bf16[2496,128]{1,0:T(8,128)(2,1)}, bf16[2496,128]{1,0:T(8,128)(2,1)}, u32[]{:S(2)}, u32[]{:S(2)}) collective-permute-start(bf16[2496,128]{1,0:T(8,128)(2,1)} %collective-permute-done.12.refs_3_), channel_id=1, source_target_pairs={{0,2},{1,3},{4,0},{5,1},{8,4},{9,5},{12,8},{13,9},{14,12},{15,13},... | collective-permute-start | bytes 1916936 | tf_op jit(solution)/shard_map/ppermute | solution.py:39
  78.6 18.2 %copy-start.10 = (bf16[2496,256]{1,0:T(8,128)(2,1)}, bf16[2496,256]{1,0:T(8,128)(2,1)S(1)}, u32[]{:S(2)}) copy-start(bf16[2496,256]{1,0:T(8,128)(2,1)S(1)} %collective-permute-done.1.refs_0_) | copy-start | bytes 3833860
  78.7 29.0 %collective-permute-start.2 = (bf16[1248,256]{1,0:T(8,128)(2,1)S(1)}, bf16[1248,256]{1,0:T(8,128)(2,1)S(1)}, u32[]{:S(2)}, u32[]{:S(2)}) collective-permute-start(bf16[1248,256]{1,0:T(8,128)(2,1)S(1)} %get-tuple-element.41), channel_id=1, source_target_pairs={{0,4},{1,5},{4,8},{5,9},{8,12},{9,13},{12,14},{13,15},{14,10},{15,... | collective-permute-start | bytes 1916936 | tf_op jit(solution)/shard_map/ppermute | solution.py:39
  81.6 27.6 %collective-permute-start.6 = (bf16[1248,256]{1,0:T(8,128)(2,1)S(1)}, bf16[1248,256]{1,0:T(8,128)(2,1)S(1)}, u32[]{:S(2)}, u32[]{:S(2)}) collective-permute-start(bf16[1248,256]{1,0:T(8,128)(2,1)S(1)} %get-tuple-element.39), channel_id=1, source_target_pairs={{0,2},{1,3},{4,0},{5,1},{8,4},{9,5},{12,8},{13,9},{14,12},{15,13},... | collective-permute-start | bytes 1916936 | tf_op jit(solution)/shard_map/ppermute | solution.py:39
  96.8 36.4 %collective-permute-start.8 = (bf16[1248,256]{1,0:T(8,128)(2,1)S(1)}, bf16[1248,256]{1,0:T(8,128)(2,1)S(1)}, u32[]{:S(2)}, u32[]{:S(2)}) collective-permute-start(bf16[1248,256]{1,0:T(8,128)(2,1)S(1)} %get-tuple-element.40), channel_id=1, source_target_pairs={{0,4},{1,5},{4,8},{5,9},{8,12},{9,13},{12,14},{13,15},{14,10},{15,... | collective-permute-start | bytes 1916936 | tf_op jit(solution)/shard_map/ppermute | solution.py:39
  98.5 36.3 %collective-permute-start.9 = (bf16[1248,256]{1,0:T(8,128)(2,1)S(1)}, bf16[1248,256]{1,0:T(8,128)(2,1)S(1)}, u32[]{:S(2)}, u32[]{:S(2)}) collective-permute-start(bf16[1248,256]{1,0:T(8,128)(2,1)S(1)} %get-tuple-element.38), channel_id=1, source_target_pairs={{0,2},{1,3},{4,0},{5,1},{8,4},{9,5},{12,8},{13,9},{14,12},{15,13},... | collective-permute-start | bytes 1916936 | tf_op jit(solution)/shard_map/ppermute | solution.py:39
  107.7 34.8 %collective-permute-start.3 = (bf16[1248,256]{1,0:T(8,128)(2,1)S(1)}, bf16[1248,256]{1,0:T(8,128)(2,1)S(1)}, u32[]{:S(2)}, u32[]{:S(2)}) collective-permute-start(bf16[1248,256]{1,0:T(8,128)(2,1)S(1)} %collective-permute-done.2.refs_0_), channel_id=1, source_target_pairs={{0,4},{1,5},{4,8},{5,9},{8,12},{9,13},{12,14},{13,15},{14,10},{15,... | collective-permute-start | bytes 1916936 | tf_op jit(solution)/shard_map/ppermute | solution.py:39
  109.2 33.3 %collective-permute-start.7 = (bf16[1248,256]{1,0:T(8,128)(2,1)S(1)}, bf16[1248,256]{1,0:T(8,128)(2,1)S(1)}, u32[]{:S(2)}, u32[]{:S(2)}) collective-permute-start(bf16[1248,256]{1,0:T(8,128)(2,1)S(1)} %collective-permute-done.6.refs_1_), channel_id=1, source_target_pairs={{0,2},{1,3},{4,0},{5,1},{8,4},{9,5},{12,8},{13,9},{14,12},{15,13},... | collective-permute-start | bytes 1916936 | tf_op jit(solution)/shard_map/ppermute | solution.py:39
  109.7 1.3 copy-start.11
  111.1 31.5 %slice-start = ((s8[5111808]{0:T(1024)(128)(4,1)}), s8[917504]{0:T(1024)(128)(4,1)S(1)}, s32[]{:S(2)}) async-start(s8[5111808]{0:T(1024)(128)(4,1)} %bitcast.5), calls=%async_computation | async-start | bytes 1835008
  111.1 31.5 %slice-start.4 = ((s8[5111808]{0:T(1024)(128)(4,1)}), s8[4194304]{0:T(1024)(128)(4,1)S(1)}, s32[]{:S(2)}) async-start(s8[5111808]{0:T(1024)(128)(4,1)} %bitcast.9), calls=%async_computation.4 | async-start | bytes 8388608
  125.6 17.0 %slice-start.1 = ((s8[5111808]{0:T(1024)(128)(4,1)}), s8[4194304]{0:T(1024)(128)(4,1)S(1)}, s32[]{:S(2)}) async-start(s8[5111808]{0:T(1024)(128)(4,1)} %bitcast.5), calls=%async_computation.1 | async-start | bytes 8388608
  125.6 17.0 %slice-start.5 = ((s8[5111808]{0:T(1024)(128)(4,1)}), s8[917504]{0:T(1024)(128)(4,1)S(1)}, s32[]{:S(2)}) async-start(s8[5111808]{0:T(1024)(128)(4,1)} %bitcast.9), calls=%async_computation.5 | async-start | bytes 1835008
  133.2 21.6 %collective-permute-start.17 = (bf16[2496,128]{1,0:T(8,128)(2,1)}, bf16[2496,128]{1,0:T(8,128)(2,1)}, u32[]{:S(2)}, u32[]{:S(2)}) collective-permute-start(bf16[2496,128]{1,0:T(8,128)(2,1)} %collective-permute-done.11.refs_1_), channel_id=1, source_target_pairs={{0,4},{1,5},{4,8},{5,9},{8,12},{9,13},{12,14},{13,15},{14,10},{15,... | collective-permute-start | bytes 1916936 | tf_op jit(solution)/shard_map/ppermute | solution.py:39
  134.8 22.6 %collective-permute-start.19 = (bf16[2496,128]{1,0:T(8,128)(2,1)}, bf16[2496,128]{1,0:T(8,128)(2,1)}, u32[]{:S(2)}, u32[]{:S(2)}) collective-permute-start(bf16[2496,128]{1,0:T(8,128)(2,1)} %collective-permute-done.13.refs_3_), channel_id=1, source_target_pairs={{0,2},{1,3},{4,0},{5,1},{8,4},{9,5},{12,8},{13,9},{14,12},{15,13},... | collective-permute-start | bytes 1916936 | tf_op jit(solution)/shard_map/ppermute | solution.py:39
  142.6 4.0 %copy-start.13 = (bf16[1024]{0:T(1024)(128)(2,1)S(1)}, bf16[1024]{0:T(1024)(128)(2,1)}, u32[]{:S(2)}) copy-start(bf16[1024]{0:T(1024)(128)(2,1)} %param.8) | copy-start | bytes 6148
  146.6 25.2 %collective-permute-start.14 = (bf16[256,2048]{1,0:T(8,128)(2,1)}, bf16[256,2048]{1,0:T(8,128)(2,1)}, u32[]{:S(2)}, u32[]{:S(2)}) collective-permute-start(bf16[256,2048]{1,0:T(8,128)(2,1)} %shard_map.68.a), channel_id=1, source_target_pairs={{0,1},{1,0},{2,3},{3,2},{4,5},{5,4},{6,7},{7,6},{8,9},{9,8},{10,11... | collective-permute-start | bytes 3145736 | tf_op jit(solution)/shard_map/ppermute | solution.py:44
  146.6 8.2 %collective-permute-start.16 = (bf16[1024]{0:T(1024)(128)(2,1)S(1)}, bf16[1024]{0:T(1024)(128)(2,1)S(1)}, u32[]{:S(2)}, u32[]{:S(2)}) collective-permute-start(bf16[1024]{0:T(1024)(128)(2,1)S(1)} %copy-done.13), channel_id=1, source_target_pairs={{0,1},{1,0},{2,3},{3,2},{4,5},{5,4},{6,7},{7,6},{8,9},{9,8},{10,11... | collective-permute-start | bytes 6152 | tf_op jit(solution)/shard_map/ppermute | solution.py:44
  147.1 12.0 %copy-start.12 = (bf16[1024,384]{0,1:T(8,128)(2,1)S(1)}, bf16[1024,384]{0,1:T(8,128)(2,1)}, u32[]{:S(2)}) copy-start(bf16[1024,384]{0,1:T(8,128)(2,1)} %copy.7) | copy-start | bytes 2359300
  155.8 21.4 %collective-permute-start.18 = (bf16[1248,128]{1,0:T(8,128)(2,1)S(1)}, bf16[1248,128]{1,0:T(8,128)(2,1)S(1)}, u32[]{:S(2)}, u32[]{:S(2)}) collective-permute-start(bf16[1248,128]{1,0:T(8,128)(2,1)S(1)} %slice.28), channel_id=1, source_target_pairs={{0,4},{1,5},{4,8},{5,9},{8,12},{9,13},{12,14},{13,15},{14,10},{15,... | collective-permute-start | bytes 958472 | tf_op jit(solution)/shard_map/ppermute | solution.py:39
  158.4 18.8 %collective-permute-start.20 = (bf16[1248,128]{1,0:T(8,128)(2,1)S(1)}, bf16[1248,128]{1,0:T(8,128)(2,1)S(1)}, u32[]{:S(2)}, u32[]{:S(2)}) collective-permute-start(bf16[1248,128]{1,0:T(8,128)(2,1)S(1)} %slice.29), channel_id=1, source_target_pairs={{0,2},{1,3},{4,0},{5,1},{8,4},{9,5},{12,8},{13,9},{14,12},{15,13},... | collective-permute-start | bytes 958472 | tf_op jit(solution)/shard_map/ppermute | solution.py:39
  159.1 18.1 %slice-start.2 = ((s8[5111808]{0:T(1024)(128)(4,1)}), s8[917504]{0:T(1024)(128)(4,1)S(1)}, s32[]{:S(2)}) async-start(s8[5111808]{0:T(1024)(128)(4,1)} %bitcast.7), calls=%async_computation.2 | async-start | bytes 1835008
  159.1 18.1 %slice-start.6 = ((s8[5111808]{0:T(1024)(128)(4,1)}), s8[4194304]{0:T(1024)(128)(4,1)S(1)}, s32[]{:S(2)}) async-start(s8[5111808]{0:T(1024)(128)(4,1)} %bitcast.11), calls=%async_computation.6 | async-start | bytes 8388608
  161.1 10.7 %copy-start.2 = (bf16[2048,640]{1,0:T(8,128)(2,1)S(1)}, bf16[2048,640]{1,0:T(8,128)(2,1)}, u32[]{:S(2)}) copy-start(bf16[2048,640]{1,0:T(8,128)(2,1)} %get-tuple-element.22.w) | copy-start | bytes 7864324
  161.1 16.1 %slice-start.3 = ((s8[5111808]{0:T(1024)(128)(4,1)}), s8[4194304]{0:T(1024)(128)(4,1)S(1)}, s32[]{:S(2)}) async-start(s8[5111808]{0:T(1024)(128)(4,1)} %bitcast.7), calls=%async_computation.3 | async-start | bytes 8388608
  161.1 16.1 %slice-start.7 = ((s8[5111808]{0:T(1024)(128)(4,1)}), s8[917504]{0:T(1024)(128)(4,1)S(1)}, s32[]{:S(2)}) async-start(s8[5111808]{0:T(1024)(128)(4,1)} %bitcast.11), calls=%async_computation.7 | async-start | bytes 1835008
  175.6 3.3 %copy-start = (bf16[2048,640]{1,0:T(8,128)(2,1)S(1)}, bf16[2048,640]{1,0:T(8,128)(2,1)}, u32[]{:S(2)}) copy-start(bf16[2048,640]{1,0:T(8,128)(2,1)} %get-tuple-element.32.refs_1_.refs_2_) | copy-start | bytes 7864324
  175.6 9.4 %collective-permute-start.22 = (bf16[264,640]{1,0:T(8,128)(2,1)S(1)}, bf16[264,640]{1,0:T(8,128)(2,1)S(1)}, u32[]{:S(2)}, u32[]{:S(2)}) collective-permute-start(bf16[264,640]{1,0:T(8,128)(2,1)S(1)} %get-tuple-element.28), channel_id=1, source_target_pairs={{0,4},{1,5},{4,8},{5,9},{8,12},{9,13},{12,14},{13,15},{14,10},{15,... | collective-permute-start | bytes 1013768 | tf_op jit(solution)/shard_map/ppermute | solution.py:39
  178.8 6.2 %copy-start.1 = (bf16[2048,640]{1,0:T(8,128)(2,1)S(1)}, bf16[2048,640]{1,0:T(8,128)(2,1)}, u32[]{:S(2)}) copy-start(bf16[2048,640]{1,0:T(8,128)(2,1)} %get-tuple-element.29.refs_2_.refs_1_) | copy-start | bytes 7864324
  178.8 8.7 %collective-permute-start.21 = (bf16[128,2048]{1,0:T(8,128)(2,1)S(1)}, bf16[128,2048]{1,0:T(8,128)(2,1)S(1)}, u32[]{:S(2)}, u32[]{:S(2)}) collective-permute-start(bf16[128,2048]{1,0:T(8,128)(2,1)S(1)} %shard_map.70.a), channel_id=1, source_target_pairs={{0,1},{1,0},{2,3},{3,2},{4,5},{5,4},{6,7},{7,6},{8,9},{9,8},{10,11... | collective-permute-start | bytes 1572872 | tf_op jit(solution)/shard_map/ppermute | solution.py:44
  179.9 17.1 %collective-permute-start.26 = (bf16[264,640]{1,0:T(8,128)(2,1)S(1)}, bf16[264,640]{1,0:T(8,128)(2,1)S(1)}, u32[]{:S(2)}, u32[]{:S(2)}) collective-permute-start(bf16[264,640]{1,0:T(8,128)(2,1)S(1)} %shard_map.77), channel_id=1, source_target_pairs={{0,2},{1,3},{4,0},{5,1},{8,4},{9,5},{12,8},{13,9},{14,12},{15,13},... | collective-permute-start | bytes 1013768 | tf_op jit(solution)/shard_map/ppermute | solution.py:39
  186.0 15.3 %collective-permute-start.23 = (bf16[264,640]{1,0:T(8,128)(2,1)S(1)}, bf16[264,640]{1,0:T(8,128)(2,1)S(1)}, u32[]{:S(2)}, u32[]{:S(2)}) collective-permute-start(bf16[264,640]{1,0:T(8,128)(2,1)S(1)} %shard_map.74), channel_id=1, source_target_pairs={{0,4},{1,5},{4,8},{5,9},{8,12},{9,13},{12,14},{13,15},{14,10},{15,... | collective-permute-start | bytes 1013768 | tf_op jit(solution)/shard_map/ppermute | solution.py:39
  188.8 16.5 %collective-permute-start.29 = (bf16[136,640]{1,0:T(8,128)(2,1)S(1)}, bf16[136,640]{1,0:T(8,128)(2,1)S(1)}, u32[]{:S(2)}, u32[]{:S(2)}) collective-permute-start(bf16[136,640]{1,0:T(8,128)(2,1)S(1)} %get-tuple-element.37), channel_id=1, source_target_pairs={{0,2},{1,3},{4,0},{5,1},{8,4},{9,5},{12,8},{13,9},{14,12},{15,13},... | collective-permute-start | bytes 522248 | tf_op jit(solution)/shard_map/ppermute | solution.py:39
  197.0 1.7 copy-start.7
  198.8 2.5 %copy-start.9 = (bf16[2048,640]{1,0:T(8,128)(2,1)S(1)}, bf16[2048,640]{1,0:T(8,128)(2,1)}, u32[]{:S(2)}) copy-start(bf16[2048,640]{1,0:T(8,128)(2,1)} %get-tuple-element.30.refs_2_) | copy-start | bytes 7864324
  199.8 17.3 %collective-permute-start.27 = (bf16[264,640]{1,0:T(8,128)(2,1)S(1)}, bf16[264,640]{1,0:T(8,128)(2,1)S(1)}, u32[]{:S(2)}, u32[]{:S(2)}) collective-permute-start(bf16[264,640]{1,0:T(8,128)(2,1)S(1)} %shard_map.78), channel_id=1, source_target_pairs={{0,2},{1,3},{4,0},{5,1},{8,4},{9,5},{12,8},{13,9},{14,12},{15,13},... | collective-permute-start | bytes 1013768 | tf_op jit(solution)/shard_map/ppermute | solution.py:39
  202.3 18.1 %collective-permute-start.24 = (bf16[264,640]{1,0:T(8,128)(2,1)S(1)}, bf16[264,640]{1,0:T(8,128)(2,1)S(1)}, u32[]{:S(2)}, u32[]{:S(2)}) collective-permute-start(bf16[264,640]{1,0:T(8,128)(2,1)S(1)} %shard_map.75), channel_id=1, source_target_pairs={{0,4},{1,5},{4,8},{5,9},{8,12},{9,13},{12,14},{13,15},{14,10},{15,... | collective-permute-start | bytes 1013768 | tf_op jit(solution)/shard_map/ppermute | solution.py:39
  203.7 10.0 %collective-permute-start.33 = (bf16[136,640]{1,0:T(8,128)(2,1)S(1)}, bf16[136,640]{1,0:T(8,128)(2,1)S(1)}, u32[]{:S(2)}, u32[]{:S(2)}) collective-permute-start(bf16[136,640]{1,0:T(8,128)(2,1)S(1)} %shard_map.84), channel_id=1, source_target_pairs={{0,4},{1,5},{4,8},{5,9},{8,12},{9,13},{12,14},{13,15},{14,10},{15,... | collective-permute-start | bytes 522248 | tf_op jit(solution)/shard_map/ppermute | solution.py:39
  205.9 9.5 %collective-permute-start.30 = (bf16[136,640]{1,0:T(8,128)(2,1)S(1)}, bf16[136,640]{1,0:T(8,128)(2,1)S(1)}, u32[]{:S(2)}, u32[]{:S(2)}) collective-permute-start(bf16[136,640]{1,0:T(8,128)(2,1)S(1)} %shard_map.81), channel_id=1, source_target_pairs={{0,2},{1,3},{4,0},{5,1},{8,4},{9,5},{12,8},{13,9},{14,12},{15,13},... | collective-permute-start | bytes 522248 | tf_op jit(solution)/shard_map/ppermute | solution.py:39
  211.0 4.3 %copy-start.8 = (bf16[2048,640]{1,0:T(8,128)(2,1)S(1)}, bf16[2048,640]{1,0:T(8,128)(2,1)}, u32[]{:S(2)}) copy-start(bf16[2048,640]{1,0:T(8,128)(2,1)} %get-tuple-element.33.refs_2_) | copy-start | bytes 7864324
  214.3 2.8 %copy-start.6 = (bf16[2048,640]{1,0:T(8,128)(2,1)S(1)}, bf16[2048,640]{1,0:T(8,128)(2,1)}, u32[]{:S(2)}) copy-start(bf16[2048,640]{1,0:T(8,128)(2,1)} %get-tuple-element.34.refs_2_) | copy-start | bytes 7864324
  214.3 8.3 %collective-permute-start.34 = (bf16[136,640]{1,0:T(8,128)(2,1)S(1)}, bf16[136,640]{1,0:T(8,128)(2,1)S(1)}, u32[]{:S(2)}, u32[]{:S(2)}) collective-permute-start(bf16[136,640]{1,0:T(8,128)(2,1)S(1)} %shard_map.85), channel_id=1, source_target_pairs={{0,4},{1,5},{4,8},{5,9},{8,12},{9,13},{12,14},{13,15},{14,10},{15,... | collective-permute-start | bytes 522248 | tf_op jit(solution)/shard_map/ppermute | solution.py:39
  216.0 4.4 %copy-start.3 = (bf16[2048,640]{1,0:T(8,128)(2,1)S(1)}, bf16[2048,640]{1,0:T(8,128)(2,1)}, u32[]{:S(2)}) copy-start(bf16[2048,640]{1,0:T(8,128)(2,1)} %get-tuple-element.31.refs_2_) | copy-start | bytes 7864324
  216.0 8.9 %collective-permute-start.31 = (bf16[136,640]{1,0:T(8,128)(2,1)S(1)}, bf16[136,640]{1,0:T(8,128)(2,1)S(1)}, u32[]{:S(2)}, u32[]{:S(2)}) collective-permute-start(bf16[136,640]{1,0:T(8,128)(2,1)S(1)} %shard_map.82), channel_id=1, source_target_pairs={{0,2},{1,3},{4,0},{5,1},{8,4},{9,5},{12,8},{13,9},{14,12},{15,13},... | collective-permute-start | bytes 522248 | tf_op jit(solution)/shard_map/ppermute | solution.py:39
  218.8 13.3 %collective-permute-start.28 = (bf16[264,640]{1,0:T(8,128)(2,1)}, bf16[264,640]{1,0:T(8,128)(2,1)S(1)}, u32[]{:S(2)}, u32[]{:S(2)}) collective-permute-start(bf16[264,640]{1,0:T(8,128)(2,1)} %shard_map.79), channel_id=1, source_target_pairs={{0,2},{1,3},{4,0},{5,1},{8,4},{9,5},{12,8},{13,9},{14,12},{15,13},... | collective-permute-start | bytes 1013768 | tf_op jit(solution)/shard_map/ppermute | solution.py:39
  222.1 10.0 %collective-permute-start.25 = (bf16[264,640]{1,0:T(8,128)(2,1)}, bf16[264,640]{1,0:T(8,128)(2,1)}, u32[]{:S(2)}, u32[]{:S(2)}) collective-permute-start(bf16[264,640]{1,0:T(8,128)(2,1)} %shard_map.76), channel_id=1, source_target_pairs={{0,4},{1,5},{4,8},{5,9},{8,12},{9,13},{12,14},{13,15},{14,10},{15,... | collective-permute-start | bytes 1013768 | tf_op jit(solution)/shard_map/ppermute | solution.py:39
  223.8 8.2 %collective-permute-start.35 = (bf16[136,640]{1,0:T(8,128)(2,1)}, bf16[136,640]{1,0:T(8,128)(2,1)}, u32[]{:S(2)}, u32[]{:S(2)}) collective-permute-start(bf16[136,640]{1,0:T(8,128)(2,1)} %shard_map.86), channel_id=1, source_target_pairs={{0,4},{1,5},{4,8},{5,9},{8,12},{9,13},{12,14},{13,15},{14,10},{15,... | collective-permute-start | bytes 522248 | tf_op jit(solution)/shard_map/ppermute | solution.py:39
  226.1 6.0 %collective-permute-start.32 = (bf16[136,640]{1,0:T(8,128)(2,1)}, bf16[136,640]{1,0:T(8,128)(2,1)}, u32[]{:S(2)}, u32[]{:S(2)}) collective-permute-start(bf16[136,640]{1,0:T(8,128)(2,1)} %shard_map.83), channel_id=1, source_target_pairs={{0,2},{1,3},{4,0},{5,1},{8,4},{9,5},{12,8},{13,9},{14,12},{15,13},... | collective-permute-start | bytes 522248 | tf_op jit(solution)/shard_map/ppermute | solution.py:39
  227.1 1.7 copy-start.4
  228.9 1.7 copy-start.5

commit v2 on v1

--- a/solution.py
+++ b/solution.py
@@ -110,31 +110,33 @@
     )(table, *operands)
 
 
-def last_step(acc, pieces, weights, out_type):
+def last_step(acc, low, pieces, weights, out_type, limit):
     count = len(pieces)
-    size, width = acc.shape
+    flat = [weight for several in weights for weight in several]
+    owner = [(j, i) for j, several in enumerate(weights) for i in range(len(several))]
+    size, width = pieces[0].shape[1], acc.shape[1]
+    rows = flat[0].shape[0]
     block = min(width, 512)
 
     def body(*refs):
-        piece_refs, weight_refs = refs[:count], refs[count : 2 * count]
-        total_ref, out = refs[2 * count :]
-        turned = [piece[...].T for piece in piece_refs]
+        piece_refs, weight_refs = refs[:count], refs[count : count + len(flat)]
+        total_ref, out = refs[count + len(flat) :]
+        turned = [piece_refs[j][i * rows : (i + 1) * rows, :].T for j, i in owner]
         for at in range(0, width, block):
             columns = slice(at, at + block)
-            total = total_ref[:, columns]
-            for rows, weight in zip(turned, weight_refs):
+            total = total_ref[low : low + size, columns]
+            for part, weight in zip(turned, weight_refs):
                 total = total + jnp.dot(
-                    rows, weight[:, columns], preferred_element_type=jnp.float32
+                    part, weight[:, columns], preferred_element_type=jnp.float32
                 )
             out[:, columns] = total.astype(out.dtype)
 
-    flops = 2 * size * width * sum(piece.shape[0] for piece in pieces)
     return small_call(
         body,
-        list(pieces) + list(weights) + [acc],
+        list(pieces) + flat + [acc],
         jax.ShapeDtypeStruct((size, width), out_type),
-        flops,
-        limit=8,
+        2 * size * width * rows * len(flat),
+        limit=limit,
     )
 
 
@@ -444,6 +446,18 @@
     for far in ((4, 3, 5), (2, 6, 1), (7, 0)):
         blocks = regrouped(table, qkv_tile, far, (width, columns), pick_of)
         weights.update(zip(far, blocks))
+    near_rows = []
+    if split:
+        for distance in (XS - near, near):
+            near_rows.append(
+                regrouped(
+                    table,
+                    half_tiles,
+                    [(distance, h) for h in range(2)],
+                    (half_rows, width),
+                    lambda table_ref, pick: table_ref[pick[0]] * 2 + pick[1],
+                )
+            )
     far_rows = regrouped(
         table,
         half_tiles,
@@ -465,10 +479,13 @@
                 sides = [([up[h]], -near, h), ([down[1 - h]], near, 1 - h)]
                 part = down_step(table, part, start, sides, half_tiles)
                 start = 0
+        elif split:
+            part = last_step(acc, low, [up, down], near_rows, jnp.float32, 8)
         else:
             sides = [([up], -near, 0), ([down], near, 0)]
             part = down_step(table, acc, low, sides, chunk_tiles)
-        sums.append(last_step(part, [ups[g][FAR], downs[g][FAR]], far_rows, jnp.bfloat16))
+        sides = [ups[g][FAR], downs[g][FAR]]
+        sums.append(last_step(part, 0, sides, [[w] for w in far_rows], jnp.bfloat16, 8))
 
     carry = columns >= max(high - low for low, high in bounds)
     blocks, parts = [], []

time: 235 us -> 257 us (1.094)
  local copies, waits for them, and re-layouts: 10.6 us -> 21.3 us
  Pallas kernels: 122 us -> 132 us
    pallas_call x4 -> x6, Pallas kernels: 28.1 us -> 44.5 us  [regrouped(): pl.pallas_call(body, in_specs=[IN_SMEM, in_hbm], out_specs=[in_hbm] * cou...]
    unnamed x45 -> x51, local copies, waits for them, and re-layouts: 7.14 us -> 17.9 us
    pallas_call x6 -> x5, Pallas kernels: 63 us -> 52.4 us  [down_step(): pl.pallas_call(body, grid_spec=pltpu.PrefetchScalarGridSpec(num_scalar_pr...]
    pallas_call x20 -> x21, Pallas kernels: 27.9 us -> 32.3 us  [small_call(): pl.pallas_call(body, in_specs=[IN_SMEM] * smem + [IN_VMEM] * (len(operand...]
where the time goes in v2:
time: 257 us; the launch traced here: 256 us
  Pallas kernels  132 us (51%)
  waiting for transfers between devices  63.5 us (25%)
  starting transfers between devices  35.5 us (14%)
  local copies, waits for them, and re-layouts  21.3 us (8%)
    ppermute x32, waiting for transfers between devices, moved(): return lax.ppermute(value, 'gx', route)  63.5 us
    pallas_call x5, Pallas kernels, down_step(): pl.pallas_call(body, grid_spec=pltpu.PrefetchScalarGridSpec(num_scalar_pr...  52.4 us
    pallas_call x6, Pallas kernels, regrouped(): pl.pallas_call(body, in_specs=[IN_SMEM, in_hbm], out_specs=[in_hbm] * cou...  44.5 us
    ppermute x32, starting transfers between devices, moved(): return lax.ppermute(value, 'gx', route)  35 us
    pallas_call x21, Pallas kernels, small_call(): pl.pallas_call(body, in_specs=[IN_SMEM] * smem + [IN_VMEM] * (len(operand...  32.3 us
    unnamed x51, local copies, waits for them, and re-layouts  17.9 us
  transfers between devices with their start and end apart: 36, of which 6 were waited for; matrix products, arithmetic and copies ran while one was open for 3% of the time, Pallas kernels for 50%

profile of v2, /device:TPU:0, one launch (start us, length us, event | category | flops | bytes accessed | tf_op | source)
XLA Modules:
  0.0 255.8 jit_solution(3936485297959823882)
XLA Ops:
  0.6 1.4 token_slice.2.refs_0_
  2.1 3.1 %collective-permute-start = (bf16[2496,256]{1,0:T(8,128)(2,1)S(1)}, bf16[2496,256]{1,0:T(8,128)(2,1)}, u32[]{:S(2)}, u32[]{:S(2)}) collective-permute-start(bf16[2496,256]{1,0:T(8,128)(2,1)S(1)} %token_slice.2.refs_0_), channel_id=1, source_target_pairs={{0,4},{1,5},{4,8},{5,9},{8,12},{9,13},{12,14},{13,15},{14,10},{15,... | collective-permute-start | bytes 3833864 | tf_op jit(solution)/shard_map/ppermute | solution.py:39
  5.2 28.1 %collective-permute-done.refs_0_ = bf16[2496,256]{1,0:T(8,128)(2,1)} collective-permute-done((bf16[2496,256]{1,0:T(8,128)(2,1)S(1)}, bf16[2496,256]{1,0:T(8,128)(2,1)}, u32[]{:S(2)}, u32[]{:S(2)}) %collective-permute-start) | collective-permute-done | bytes 1277984 | tf_op jit(solution)/shard_map/ppermute | solution.py:39
  33.3 1.8 collective-permute-start.1
  35.3 1.2 token_slice.3.refs_1_
  36.6 1.8 collective-permute-start.10
  38.7 2.3 copy.7
  41.0 8.2 %regrouped.6 = (bf16[1248,2048]{1,0:T(8,128)(2,1)}, bf16[1248,2048]{1,0:T(8,128)(2,1)}) custom-call(s32[8]{0:T(128)S(1)} %compare_select_fusion.2.table_ref, bf16[16,1248,2048]{2,1,0:T(8,128)(2,1)} %bitcast.1.source_ref.refs_2_.refs_3_), custom_call_target="tpu_custom_call" | custom-call | bytes 20447232 | tf_op jit(solution)/shard_map/regrouped/pallas_call | solution.py:209
  49.2 8.4 %down_step.5.refs_6_ = f32[384,2048]{1,0:T(8,128)S(1)} custom-call(s32[8]{0:T(128)S(1)} %compare_select_fusion.2.table_ref, bf16[2496,256]{1,0:T(8,128)(2,1)S(1)} %token_slice.2.refs_0_, bf16[2496,128]{1,0:T(8,128)(2,1)S(1)} %token_slice.3.refs_1_, bf16[8,2496,2048]{2,1,0:T(8,128)(2,1)} %bitcast.2.refs_2_.refs_4_.refs_5_), custom_call_target="tpu_custom_call" | custom-call | flops 3925868544 | bytes 18432000 | tf_op jit(solution)/shard_map/down_step/pallas_call | solution.py:93
  57.6 19.0 %collective-permute-done.10.refs_1_ = bf16[2496,128]{1,0:T(8,128)(2,1)} collective-permute-done((bf16[2496,128]{1,0:T(8,128)(2,1)S(1)}, bf16[2496,128]{1,0:T(8,128)(2,1)}, u32[]{:S(2)}, u32[]{:S(2)}) %collective-permute-start.10) | collective-permute-done | bytes 639008 | tf_op jit(solution)/shard_map/ppermute | solution.py:39
  76.6 1.5 collective-permute-start.11
  78.7 1.6 collective-permute-start.2
  80.3 1.4 fusion.2
  82.2 14.6 %down_step.6.refs_6_ = f32[384,2048]{1,0:T(8,128)S(1)} custom-call(s32[8]{0:T(128)S(1)} %compare_select_fusion.2.table_ref, bf16[2496,256]{1,0:T(8,128)(2,1)} %collective-permute-done.refs_0_, bf16[2496,128]{1,0:T(8,128)(2,1)} %collective-permute-done.10.refs_1_, bf16[2496,256]{1,0:T(8,128)(2,1)} %collective-permute-done.4.refs_2_, ...), custom_call_target="tpu_custom_call" | custom-call | flops 7851737088 | bytes 30572544 | tf_op jit(solution)/shard_map/down_step/pallas_call | solution.py:93
  96.8 1.6 collective-permute-start.8
  98.9 8.8 %collective-permute-done.2.refs_0_ = bf16[1248,256]{1,0:T(8,128)(2,1)S(1)} collective-permute-done((bf16[1248,256]{1,0:T(8,128)(2,1)S(1)}, bf16[1248,256]{1,0:T(8,128)(2,1)S(1)}, u32[]{:S(2)}, u32[]{:S(2)}) %collective-permute-start.2) | collective-permute-done | bytes 639008 | tf_op jit(solution)/shard_map/ppermute | solution.py:39
  107.7 1.5 collective-permute-start.3
  109.7 1.3 copy-done.11
  111.1 14.5 %down_step.7.refs_4_.refs_6_ = f32[384,2048]{1,0:T(8,128)S(1)} custom-call(s32[8]{0:T(128)S(1)} %compare_select_fusion.2.table_ref, bf16[2496,256]{1,0:T(8,128)(2,1)S(1)} %copy-done.11, bf16[2496,128]{1,0:T(8,128)(2,1)} %collective-permute-done.11.refs_1_, bf16[2496,256]{1,0:T(8,128)(2,1)} %collective-permute-done.5.refs_2_, ...), custom_call_target="tpu_custom_call" | custom-call | flops 7851737088 | bytes 30572544 | tf_op jit(solution)/shard_map/down_step/pallas_call | solution.py:93
  125.6 7.6 %down_step.8.refs_4_ = f32[256,2048]{1,0:T(8,128)S(1)} custom-call(s32[8]{0:T(128)S(1)} %compare_select_fusion.2.table_ref, bf16[1248,256]{1,0:T(8,128)(2,1)S(1)} %collective-permute-done.2.refs_0_, bf16[1248,256]{1,0:T(8,128)(2,1)S(1)} %collective-permute-done.6.refs_1_, bf16[16,1248,2048]{2,1,0:T(8,128)(2,1)} %bitcast.1.source_ref.refs_2_.refs_3_, ...), custom_call_target="tpu_custom_call" | custom-call | flops 2617245696 | bytes 15695872 | tf_op jit(solution)/shard_map/down_step/pallas_call | solution.py:93
  133.2 1.6 collective-permute-start.17
  135.3 7.3 %down_step.9.refs_4_ = f32[256,2048]{1,0:T(8,128)S(1)} custom-call(s32[8]{0:T(128)S(1)} %compare_select_fusion.2.table_ref, bf16[1248,256]{1,0:T(8,128)(2,1)S(1)} %collective-permute-done.8.refs_0_, bf16[1248,256]{1,0:T(8,128)(2,1)S(1)} %collective-permute-done.9.refs_1_, bf16[16,1248,2048]{2,1,0:T(8,128)(2,1)} %bitcast.1.source_ref.refs_2_.refs_3_, ...), custom_call_target="tpu_custom_call" | custom-call | flops 2617245696 | bytes 15695872 | tf_op jit(solution)/shard_map/down_step/pallas_call | solution.py:93
  142.7 3.9 %shard_map.68.a = bf16[256,2048]{1,0:T(8,128)(2,1)} custom-call(bf16[1248,256]{1,0:T(8,128)(2,1)S(1)} %collective-permute-done.3.refs_0_, bf16[1248,256]{1,0:T(8,128)(2,1)S(1)} %collective-permute-done.7.refs_1_, bf16[1248,2048]{1,0:T(8,128)(2,1)S(1)} %bitcast.6, bf16[1248,2048]{1,0:T(8,128)(2,1)S(1)} %bitcast.10, f32[256,2048]{1,0:T(8,128)S(1)} %down_step.9.refs_4_), custom_call_target="tpu_custom_call" | custom-call | flops 2617245696 | bytes 13598720 | tf_op jit(solution)/shard_map/pallas_call | solution.py:228
  147.1 8.1 %regrouped.8 = (bf16[1248,2048]{1,0:T(8,128)(2,1)}, bf16[1248,2048]{1,0:T(8,128)(2,1)}) custom-call(s32[8]{0:T(128)S(1)} %compare_select_fusion.2.table_ref, bf16[16,1248,2048]{2,1,0:T(8,128)(2,1)} %bitcast.1.source_ref.refs_2_.refs_3_), custom_call_target="tpu_custom_call" | custom-call | bytes 20447232 | tf_op jit(solution)/shard_map/regrouped/pallas_call | solution.py:209
  155.2 8.2 %regrouped.9 = (bf16[1248,2048]{1,0:T(8,128)(2,1)}, bf16[1248,2048]{1,0:T(8,128)(2,1)}) custom-call(s32[8]{0:T(128)S(1)} %compare_select_fusion.2.table_ref, bf16[16,1248,2048]{2,1,0:T(8,128)(2,1)} %bitcast.1.source_ref.refs_2_.refs_3_), custom_call_target="tpu_custom_call" | custom-call | bytes 20447232 | tf_op jit(solution)/shard_map/regrouped/pallas_call | solution.py:209
  163.4 7.7 %regrouped.7 = (bf16[2048,640]{1,0:T(8,128)(2,1)}, bf16[2048,640]{1,0:T(8,128)(2,1)}, bf16[2048,640]{1,0:T(8,128)(2,1)}) custom-call(s32[8]{0:T(128)S(1)} %compare_select_fusion.2.table_ref, bf16[2048,5120]{1,0:T(8,128)(2,1)} %bitcast.13), custom_call_target="tpu_custom_call" | custom-call | bytes 15728640 | tf_op jit(solution)/shard_map/regrouped/pallas_call | solution.py:209
  171.2 1.0 slice.28
  172.2 1.6 collective-permute-start.18
  173.8 1.0 slice.29
  175.5 2.5 maximum_select_fusion.r
  178.0 2.6 %copy-done.12 = bf16[1248,2048]{1,0:T(8,128)(2,1)S(1)} copy-done((bf16[1248,2048]{1,0:T(8,128)(2,1)S(1)}, bf16[1248,2048]{1,0:T(8,128)(2,1)}, u32[]{:S(2)}) %copy-start.12) | copy-done | bytes 5111832
  180.6 3.2 %copy-done.13 = bf16[1248,2048]{1,0:T(8,128)(2,1)S(1)} copy-done((bf16[1248,2048]{1,0:T(8,128)(2,1)S(1)}, bf16[1248,2048]{1,0:T(8,128)(2,1)}, u32[]{:S(2)}) %copy-start.13) | copy-done | bytes 5111832
  183.8 2.4 copy-done.14
  186.3 2.4 copy-done.15
  188.7 4.3 %shard_map.70.refs_4_ = f32[128,2048]{1,0:T(8,128)S(1)} custom-call(bf16[2496,128]{1,0:T(8,128)(2,1)} %collective-permute-done.17.refs_0_, bf16[2496,128]{1,0:T(8,128)(2,1)} %collective-permute-done.19.refs_1_, bf16[1248,2048]{1,0:T(8,128)(2,1)S(1)} %copy-done.12, bf16[1248,2048]{1,0:T(8,128)(2,1)S(1)} %copy-done.13, bf16[1248,2048]{1,0:T(8,128)(2,1)S(1)} %copy-done.14, ...), custom_call_target="tpu_custom_call" | custom-call | flops 2617245696 | bytes 24870912 | tf_op jit(solution)/shard_map/pallas_call | solution.py:228
  193.1 3.8 %shard_map.69 = (bf16[256,2048]{1,0:T(8,128)(2,1)S(1)}, bf16[256,2048]{1,0:T(8,128)(2,1)S(1)}, f32[8,256]{1,0:T(8,128)S(1)}, bf16[264,640]{1,0:T(8,128)(2,1)S(1)}) custom-call(bf16[256,2048]{1,0:T(8,128)(2,1)} %shard_map.68.a, bf16[256,2048]{1,0:T(8,128)(2,1)} %collective-permute-done.14.b, bf16[384,2048]{1,0:T(8,128)(2,1)S(1)} %maximum_select_fusion.r, ...), custom_call_target="tpu_custom_call" | custom-call | flops 671088640 | bytes 6299648 | tf_op jit(solution)/shard_map/pallas_call | solution.py:228
  196.9 1.6 collective-permute-start.22
  198.5 1.6 shard_map.71.a
  200.2 1.0 shard_map.78
  201.8 4.4 %collective-permute-done.22.refs_0_ = bf16[264,640]{1,0:T(8,128)(2,1)S(1)} collective-permute-done((bf16[264,640]{1,0:T(8,128)(2,1)S(1)}, bf16[264,640]{1,0:T(8,128)(2,1)S(1)}, u32[]{:S(2)}, u32[]{:S(2)}) %collective-permute-start.22) | collective-permute-done | bytes 337952 | tf_op jit(solution)/shard_map/ppermute | solution.py:39
  206.2 1.0 shard_map.75
  207.2 1.6 collective-permute-start.23
  208.8 1.2 shard_map.72
  210.6 7.7 %regrouped.11 = (bf16[2048,640]{1,0:T(8,128)(2,1)}, bf16[2048,640]{1,0:T(8,128)(2,1)}, bf16[2048,640]{1,0:T(8,128)(2,1)}) custom-call(s32[8]{0:T(128)S(1)} %compare_select_fusion.2.table_ref, bf16[2048,5120]{1,0:T(8,128)(2,1)} %bitcast.14), custom_call_target="tpu_custom_call" | custom-call | bytes 15728640 | tf_op jit(solution)/shard_map/regrouped/pallas_call | solution.py:209
  218.3 1.7 copy-done.7
  220.0 1.0 shard_map.79
  221.0 1.5 collective-permute-start.27
  222.5 1.0 shard_map.76
  224.9 1.6 collective-permute-start.33
  227.6 4.6 %regrouped.10 = (bf16[2048,640]{1,0:T(8,128)(2,1)}, bf16[2048,640]{1,0:T(8,128)(2,1)}) custom-call(s32[8]{0:T(128)S(1)} %compare_select_fusion.2.table_ref, bf16[2048,5120]{1,0:T(8,128)(2,1)} %bitcast.15), custom_call_target="tpu_custom_call" | custom-call | bytes 10485760 | tf_op jit(solution)/shard_map/regrouped/pallas_call | solution.py:209
  232.3 2.6 %collective-permute-done.33.refs_0_ = bf16[136,640]{1,0:T(8,128)(2,1)S(1)} collective-permute-done((bf16[136,640]{1,0:T(8,128)(2,1)S(1)}, bf16[136,640]{1,0:T(8,128)(2,1)S(1)}, u32[]{:S(2)}, u32[]{:S(2)}) %collective-permute-start.33) | collective-permute-done | bytes 174112 | tf_op jit(solution)/shard_map/ppermute | solution.py:39
  235.5 1.3 collective-permute-start.34
  237.4 1.1 collective-permute-start.31
  238.5 1.7 shard_map.80
  240.2 1.6 collective-permute-start.28
  241.8 1.7 shard_map.77
  244.0 1.3 shard_map.87
  245.3 1.0 collective-permute-start.35
  246.3 1.3 shard_map.84
  247.6 1.0 collective-permute-start.32
  248.6 1.7 copy-done.4
  250.9 1.1 shard_map.73
  252.1 1.0 shard_map.74.refs_0_
  253.5 2.3 shard_map.88
  (106 shorter events, 10.9 us)
Async XLA Ops:
  2.1 31.2 %collective-permute-start = (bf16[2496,256]{1,0:T(8,128)(2,1)S(1)}, bf16[2496,256]{1,0:T(8,128)(2,1)}, u32[]{:S(2)}, u32[]{:S(2)}) collective-permute-start(bf16[2496,256]{1,0:T(8,128)(2,1)S(1)} %token_slice.2.refs_0_), channel_id=1, source_target_pairs={{0,4},{1,5},{4,8},{5,9},{8,12},{9,13},{12,14},{13,15},{14,10},{15,... | collective-permute-start | bytes 3833864 | tf_op jit(solution)/shard_map/ppermute | solution.py:39
  5.2 29.9 %collective-permute-start.4 = (bf16[2496,256]{1,0:T(8,128)(2,1)S(1)}, bf16[2496,256]{1,0:T(8,128)(2,1)}, u32[]{:S(2)}, u32[]{:S(2)}) collective-permute-start(bf16[2496,256]{1,0:T(8,128)(2,1)S(1)} %token_slice.2.refs_0_), channel_id=1, source_target_pairs={{0,2},{1,3},{4,0},{5,1},{8,4},{9,5},{12,8},{13,9},{14,12},{15,13},... | collective-permute-start | bytes 3833864 | tf_op jit(solution)/shard_map/ppermute | solution.py:39
  33.3 45.3 %collective-permute-start.1 = (bf16[2496,256]{1,0:T(8,128)(2,1)}, bf16[2496,256]{1,0:T(8,128)(2,1)S(1)}, u32[]{:S(2)}, u32[]{:S(2)}) collective-permute-start(bf16[2496,256]{1,0:T(8,128)(2,1)} %collective-permute-done.refs_0_), channel_id=1, source_target_pairs={{0,4},{1,5},{4,8},{5,9},{8,12},{9,13},{12,14},{13,15},{14,10},{15,... | collective-permute-start | bytes 3833864 | tf_op jit(solution)/shard_map/ppermute | solution.py:39
  35.1 45.1 %collective-permute-start.5 = (bf16[2496,256]{1,0:T(8,128)(2,1)}, bf16[2496,256]{1,0:T(8,128)(2,1)}, u32[]{:S(2)}, u32[]{:S(2)}) collective-permute-start(bf16[2496,256]{1,0:T(8,128)(2,1)} %collective-permute-done.4.refs_2_), channel_id=1, source_target_pairs={{0,2},{1,3},{4,0},{5,1},{8,4},{9,5},{12,8},{13,9},{14,12},{15,13},... | collective-permute-start | bytes 3833864 | tf_op jit(solution)/shard_map/ppermute | solution.py:39
  36.6 40.0 %collective-permute-start.10 = (bf16[2496,128]{1,0:T(8,128)(2,1)S(1)}, bf16[2496,128]{1,0:T(8,128)(2,1)}, u32[]{:S(2)}, u32[]{:S(2)}) collective-permute-start(bf16[2496,128]{1,0:T(8,128)(2,1)S(1)} %token_slice.3.refs_1_), channel_id=1, source_target_pairs={{0,4},{1,5},{4,8},{5,9},{8,12},{9,13},{12,14},{13,15},{14,10},{15,... | collective-permute-start | bytes 1916936 | tf_op jit(solution)/shard_map/ppermute | solution.py:39
  38.4 39.7 %collective-permute-start.12 = (bf16[2496,128]{1,0:T(8,128)(2,1)S(1)}, bf16[2496,128]{1,0:T(8,128)(2,1)}, u32[]{:S(2)}, u32[]{:S(2)}) collective-permute-start(bf16[2496,128]{1,0:T(8,128)(2,1)S(1)} %token_slice.3.refs_1_), channel_id=1, source_target_pairs={{0,2},{1,3},{4,0},{5,1},{8,4},{9,5},{12,8},{13,9},{14,12},{15,13},... | collective-permute-start | bytes 1916936 | tf_op jit(solution)/shard_map/ppermute | solution.py:39
  40.9 134.5 %collective-permute-start.15 = (bf16[384,1024]{1,0:T(8,128)(2,1)}, bf16[384,1024]{1,0:T(8,128)(2,1)}, u32[]{:S(2)}, u32[]{:S(2)}) collective-permute-start(bf16[384,1024]{1,0:T(8,128)(2,1)} %bitcast.16), channel_id=1, source_target_pairs={{0,1},{1,0},{2,3},{3,2},{4,5},{5,4},{6,7},{7,6},{8,9},{9,8},{10,11... | collective-permute-start | bytes 2359304 | tf_op jit(solution)/shard_map/ppermute | solution.py:44
  76.6 20.3 %collective-permute-start.11 = (bf16[2496,128]{1,0:T(8,128)(2,1)}, bf16[2496,128]{1,0:T(8,128)(2,1)}, u32[]{:S(2)}, u32[]{:S(2)}) collective-permute-start(bf16[2496,128]{1,0:T(8,128)(2,1)} %collective-permute-done.10.refs_1_), channel_id=1, source_target_pairs={{0,4},{1,5},{4,8},{5,9},{8,12},{9,13},{12,14},{13,15},{14,10},{15,... | collective-permute-start | bytes 1916936 | tf_op jit(solution)/shard_map/ppermute | solution.py:39
  78.1 20.4 %collective-permute-start.13 = (bf16[2496,128]{1,0:T(8,128)(2,1)}, bf16[2496,128]{1,0:T(8,128)(2,1)}, u32[]{:S(2)}, u32[]{:S(2)}) collective-permute-start(bf16[2496,128]{1,0:T(8,128)(2,1)} %collective-permute-done.12.refs_3_), channel_id=1, source_target_pairs={{0,2},{1,3},{4,0},{5,1},{8,4},{9,5},{12,8},{13,9},{14,12},{15,13},... | collective-permute-start | bytes 1916936 | tf_op jit(solution)/shard_map/ppermute | solution.py:39
  78.6 18.2 %copy-start.10 = (bf16[2496,256]{1,0:T(8,128)(2,1)}, bf16[2496,256]{1,0:T(8,128)(2,1)S(1)}, u32[]{:S(2)}) copy-start(bf16[2496,256]{1,0:T(8,128)(2,1)S(1)} %collective-permute-done.1.refs_0_) | copy-start | bytes 3833860
  78.7 29.0 %collective-permute-start.2 = (bf16[1248,256]{1,0:T(8,128)(2,1)S(1)}, bf16[1248,256]{1,0:T(8,128)(2,1)S(1)}, u32[]{:S(2)}, u32[]{:S(2)}) collective-permute-start(bf16[1248,256]{1,0:T(8,128)(2,1)S(1)} %get-tuple-element.49), channel_id=1, source_target_pairs={{0,4},{1,5},{4,8},{5,9},{8,12},{9,13},{12,14},{13,15},{14,10},{15,... | collective-permute-start | bytes 1916936 | tf_op jit(solution)/shard_map/ppermute | solution.py:39
  81.6 27.6 %collective-permute-start.6 = (bf16[1248,256]{1,0:T(8,128)(2,1)S(1)}, bf16[1248,256]{1,0:T(8,128)(2,1)S(1)}, u32[]{:S(2)}, u32[]{:S(2)}) collective-permute-start(bf16[1248,256]{1,0:T(8,128)(2,1)S(1)} %get-tuple-element.47), channel_id=1, source_target_pairs={{0,2},{1,3},{4,0},{5,1},{8,4},{9,5},{12,8},{13,9},{14,12},{15,13},... | collective-permute-start | bytes 1916936 | tf_op jit(solution)/shard_map/ppermute | solution.py:39
  96.8 36.4 %collective-permute-start.8 = (bf16[1248,256]{1,0:T(8,128)(2,1)S(1)}, bf16[1248,256]{1,0:T(8,128)(2,1)S(1)}, u32[]{:S(2)}, u32[]{:S(2)}) collective-permute-start(bf16[1248,256]{1,0:T(8,128)(2,1)S(1)} %get-tuple-element.48), channel_id=1, source_target_pairs={{0,4},{1,5},{4,8},{5,9},{8,12},{9,13},{12,14},{13,15},{14,10},{15,... | collective-permute-start | bytes 1916936 | tf_op jit(solution)/shard_map/ppermute | solution.py:39
  98.4 36.3 %collective-permute-start.9 = (bf16[1248,256]{1,0:T(8,128)(2,1)S(1)}, bf16[1248,256]{1,0:T(8,128)(2,1)S(1)}, u32[]{:S(2)}, u32[]{:S(2)}) collective-permute-start(bf16[1248,256]{1,0:T(8,128)(2,1)S(1)} %get-tuple-element.46), channel_id=1, source_target_pairs={{0,2},{1,3},{4,0},{5,1},{8,4},{9,5},{12,8},{13,9},{14,12},{15,13},... | collective-permute-start | bytes 1916936 | tf_op jit(solution)/shard_map/ppermute | solution.py:39
  107.7 34.8 %collective-permute-start.3 = (bf16[1248,256]{1,0:T(8,128)(2,1)S(1)}, bf16[1248,256]{1,0:T(8,128)(2,1)S(1)}, u32[]{:S(2)}, u32[]{:S(2)}) collective-permute-start(bf16[1248,256]{1,0:T(8,128)(2,1)S(1)} %collective-permute-done.2.refs_0_), channel_id=1, source_target_pairs={{0,4},{1,5},{4,8},{5,9},{8,12},{9,13},{12,14},{13,15},{14,10},{15,... | collective-permute-start | bytes 1916936 | tf_op jit(solution)/shard_map/ppermute | solution.py:39
  109.2 33.3 %collective-permute-start.7 = (bf16[1248,256]{1,0:T(8,128)(2,1)S(1)}, bf16[1248,256]{1,0:T(8,128)(2,1)S(1)}, u32[]{:S(2)}, u32[]{:S(2)}) collective-permute-start(bf16[1248,256]{1,0:T(8,128)(2,1)S(1)} %collective-permute-done.6.refs_1_), channel_id=1, source_target_pairs={{0,2},{1,3},{4,0},{5,1},{8,4},{9,5},{12,8},{13,9},{14,12},{15,13},... | collective-permute-start | bytes 1916936 | tf_op jit(solution)/shard_map/ppermute | solution.py:39
  109.7 1.3 copy-start.11
  111.1 31.5 %slice-start = ((s8[5111808]{0:T(1024)(128)(4,1)}), s8[917504]{0:T(1024)(128)(4,1)S(1)}, s32[]{:S(2)}) async-start(s8[5111808]{0:T(1024)(128)(4,1)} %bitcast.5), calls=%async_computation | async-start | bytes 1835008
  111.1 31.5 %slice-start.4 = ((s8[5111808]{0:T(1024)(128)(4,1)}), s8[4194304]{0:T(1024)(128)(4,1)S(1)}, s32[]{:S(2)}) async-start(s8[5111808]{0:T(1024)(128)(4,1)} %bitcast.9), calls=%async_computation.4 | async-start | bytes 8388608
  125.6 17.0 %slice-start.1 = ((s8[5111808]{0:T(1024)(128)(4,1)}), s8[4194304]{0:T(1024)(128)(4,1)S(1)}, s32[]{:S(2)}) async-start(s8[5111808]{0:T(1024)(128)(4,1)} %bitcast.5), calls=%async_computation.1 | async-start | bytes 8388608
  125.6 17.0 %slice-start.5 = ((s8[5111808]{0:T(1024)(128)(4,1)}), s8[917504]{0:T(1024)(128)(4,1)S(1)}, s32[]{:S(2)}) async-start(s8[5111808]{0:T(1024)(128)(4,1)} %bitcast.9), calls=%async_computation.5 | async-start | bytes 1835008
  133.2 38.0 %collective-permute-start.17 = (bf16[2496,128]{1,0:T(8,128)(2,1)}, bf16[2496,128]{1,0:T(8,128)(2,1)}, u32[]{:S(2)}, u32[]{:S(2)}) collective-permute-start(bf16[2496,128]{1,0:T(8,128)(2,1)} %collective-permute-done.11.refs_1_), channel_id=1, source_target_pairs={{0,4},{1,5},{4,8},{5,9},{8,12},{9,13},{12,14},{13,15},{14,10},{15,... | collective-permute-start | bytes 1916936 | tf_op jit(solution)/shard_map/ppermute | solution.py:39
  134.8 39.0 %collective-permute-start.19 = (bf16[2496,128]{1,0:T(8,128)(2,1)}, bf16[2496,128]{1,0:T(8,128)(2,1)}, u32[]{:S(2)}, u32[]{:S(2)}) collective-permute-start(bf16[2496,128]{1,0:T(8,128)(2,1)} %collective-permute-done.13.refs_3_), channel_id=1, source_target_pairs={{0,2},{1,3},{4,0},{5,1},{8,4},{9,5},{12,8},{13,9},{14,12},{15,13},... | collective-permute-start | bytes 1916936 | tf_op jit(solution)/shard_map/ppermute | solution.py:39
  142.6 4.0 %copy-start.16 = (bf16[1024]{0:T(1024)(128)(2,1)S(1)}, bf16[1024]{0:T(1024)(128)(2,1)}, u32[]{:S(2)}) copy-start(bf16[1024]{0:T(1024)(128)(2,1)} %param.8) | copy-start | bytes 6148
  146.6 46.5 %collective-permute-start.14 = (bf16[256,2048]{1,0:T(8,128)(2,1)}, bf16[256,2048]{1,0:T(8,128)(2,1)}, u32[]{:S(2)}, u32[]{:S(2)}) collective-permute-start(bf16[256,2048]{1,0:T(8,128)(2,1)} %shard_map.68.a), channel_id=1, source_target_pairs={{0,1},{1,0},{2,3},{3,2},{4,5},{5,4},{6,7},{7,6},{8,9},{9,8},{10,11... | collective-permute-start | bytes 3145736 | tf_op jit(solution)/shard_map/ppermute | solution.py:44
  146.6 24.5 %collective-permute-start.16 = (bf16[1024]{0:T(1024)(128)(2,1)S(1)}, bf16[1024]{0:T(1024)(128)(2,1)S(1)}, u32[]{:S(2)}, u32[]{:S(2)}) collective-permute-start(bf16[1024]{0:T(1024)(128)(2,1)S(1)} %copy-done.16), channel_id=1, source_target_pairs={{0,1},{1,0},{2,3},{3,2},{4,5},{5,4},{6,7},{7,6},{8,9},{9,8},{10,11... | collective-permute-start | bytes 6152 | tf_op jit(solution)/shard_map/ppermute | solution.py:44
  172.2 26.3 %collective-permute-start.18 = (bf16[1248,128]{1,0:T(8,128)(2,1)S(1)}, bf16[1248,128]{1,0:T(8,128)(2,1)S(1)}, u32[]{:S(2)}, u32[]{:S(2)}) collective-permute-start(bf16[1248,128]{1,0:T(8,128)(2,1)S(1)} %slice.28), channel_id=1, source_target_pairs={{0,4},{1,5},{4,8},{5,9},{8,12},{9,13},{12,14},{13,15},{14,10},{15,... | collective-permute-start | bytes 958472 | tf_op jit(solution)/shard_map/ppermute | solution.py:39
  174.7 23.7 %collective-permute-start.20 = (bf16[1248,128]{1,0:T(8,128)(2,1)S(1)}, bf16[1248,128]{1,0:T(8,128)(2,1)S(1)}, u32[]{:S(2)}, u32[]{:S(2)}) collective-permute-start(bf16[1248,128]{1,0:T(8,128)(2,1)S(1)} %slice.29), channel_id=1, source_target_pairs={{0,2},{1,3},{4,0},{5,1},{8,4},{9,5},{12,8},{13,9},{14,12},{15,13},... | collective-permute-start | bytes 958472 | tf_op jit(solution)/shard_map/ppermute | solution.py:39
  177.9 20.5 %slice-start.2 = ((s8[5111808]{0:T(1024)(128)(4,1)}), s8[4194304]{0:T(1024)(128)(4,1)S(1)}, s32[]{:S(2)}) async-start(s8[5111808]{0:T(1024)(128)(4,1)} %bitcast.7), calls=%async_computation.2 | async-start | bytes 8388608
  178.0 20.5 %slice-start.6 = ((s8[5111808]{0:T(1024)(128)(4,1)}), s8[4194304]{0:T(1024)(128)(4,1)S(1)}, s32[]{:S(2)}) async-start(s8[5111808]{0:T(1024)(128)(4,1)} %bitcast.11), calls=%async_computation.6 | async-start | bytes 8388608
  178.0 2.6 %copy-start.12 = (bf16[1248,2048]{1,0:T(8,128)(2,1)S(1)}, bf16[1248,2048]{1,0:T(8,128)(2,1)}, u32[]{:S(2)}) copy-start(bf16[1248,2048]{1,0:T(8,128)(2,1)} %get-tuple-element.28.refs_2_) | copy-start | bytes 15335428
  180.6 3.2 %copy-start.13 = (bf16[1248,2048]{1,0:T(8,128)(2,1)S(1)}, bf16[1248,2048]{1,0:T(8,128)(2,1)}, u32[]{:S(2)}) copy-start(bf16[1248,2048]{1,0:T(8,128)(2,1)} %get-tuple-element.29.refs_3_) | copy-start | bytes 15335428
  183.8 2.4 copy-start.14
  186.3 2.4 copy-start.15
  188.7 4.4 %copy-start.2 = (bf16[2048,640]{1,0:T(8,128)(2,1)S(1)}, bf16[2048,640]{1,0:T(8,128)(2,1)}, u32[]{:S(2)}) copy-start(bf16[2048,640]{1,0:T(8,128)(2,1)} %get-tuple-element.26.w) | copy-start | bytes 7864324
  188.7 9.8 %slice-start.3 = ((s8[5111808]{0:T(1024)(128)(4,1)}), s8[917504]{0:T(1024)(128)(4,1)S(1)}, s32[]{:S(2)}) async-start(s8[5111808]{0:T(1024)(128)(4,1)} %bitcast.7), calls=%async_computation.3 | async-start | bytes 1835008
  188.7 9.8 %slice-start.7 = ((s8[5111808]{0:T(1024)(128)(4,1)}), s8[917504]{0:T(1024)(128)(4,1)S(1)}, s32[]{:S(2)}) async-start(s8[5111808]{0:T(1024)(128)(4,1)} %bitcast.11), calls=%async_computation.7 | async-start | bytes 1835008
  196.9 3.3 %copy-start = (bf16[2048,640]{1,0:T(8,128)(2,1)S(1)}, bf16[2048,640]{1,0:T(8,128)(2,1)}, u32[]{:S(2)}) copy-start(bf16[2048,640]{1,0:T(8,128)(2,1)} %get-tuple-element.40.refs_1_.refs_2_) | copy-start | bytes 7864324
  196.9 9.3 %collective-permute-start.22 = (bf16[264,640]{1,0:T(8,128)(2,1)S(1)}, bf16[264,640]{1,0:T(8,128)(2,1)S(1)}, u32[]{:S(2)}, u32[]{:S(2)}) collective-permute-start(bf16[264,640]{1,0:T(8,128)(2,1)S(1)} %get-tuple-element.36), channel_id=1, source_target_pairs={{0,4},{1,5},{4,8},{5,9},{8,12},{9,13},{12,14},{13,15},{14,10},{15,... | collective-permute-start | bytes 1013768 | tf_op jit(solution)/shard_map/ppermute | solution.py:39
  200.1 6.1 %copy-start.1 = (bf16[2048,640]{1,0:T(8,128)(2,1)S(1)}, bf16[2048,640]{1,0:T(8,128)(2,1)}, u32[]{:S(2)}) copy-start(bf16[2048,640]{1,0:T(8,128)(2,1)} %get-tuple-element.37.refs_2_.refs_1_) | copy-start | bytes 7864324
  200.2 8.7 %collective-permute-start.21 = (bf16[128,2048]{1,0:T(8,128)(2,1)S(1)}, bf16[128,2048]{1,0:T(8,128)(2,1)S(1)}, u32[]{:S(2)}, u32[]{:S(2)}) collective-permute-start(bf16[128,2048]{1,0:T(8,128)(2,1)S(1)} %shard_map.71.a), channel_id=1, source_target_pairs={{0,1},{1,0},{2,3},{3,2},{4,5},{5,4},{6,7},{7,6},{8,9},{9,8},{10,11... | collective-permute-start | bytes 1572872 | tf_op jit(solution)/shard_map/ppermute | solution.py:44
  201.2 17.0 %collective-permute-start.26 = (bf16[264,640]{1,0:T(8,128)(2,1)S(1)}, bf16[264,640]{1,0:T(8,128)(2,1)S(1)}, u32[]{:S(2)}, u32[]{:S(2)}) collective-permute-start(bf16[264,640]{1,0:T(8,128)(2,1)S(1)} %shard_map.78), channel_id=1, source_target_pairs={{0,2},{1,3},{4,0},{5,1},{8,4},{9,5},{12,8},{13,9},{14,12},{15,13},... | collective-permute-start | bytes 1013768 | tf_op jit(solution)/shard_map/ppermute | solution.py:39
  207.2 15.3 %collective-permute-start.23 = (bf16[264,640]{1,0:T(8,128)(2,1)S(1)}, bf16[264,640]{1,0:T(8,128)(2,1)S(1)}, u32[]{:S(2)}, u32[]{:S(2)}) collective-permute-start(bf16[264,640]{1,0:T(8,128)(2,1)S(1)} %shard_map.75), channel_id=1, source_target_pairs={{0,4},{1,5},{4,8},{5,9},{8,12},{9,13},{12,14},{13,15},{14,10},{15,... | collective-permute-start | bytes 1013768 | tf_op jit(solution)/shard_map/ppermute | solution.py:39
  210.0 16.5 %collective-permute-start.29 = (bf16[136,640]{1,0:T(8,128)(2,1)S(1)}, bf16[136,640]{1,0:T(8,128)(2,1)S(1)}, u32[]{:S(2)}, u32[]{:S(2)}) collective-permute-start(bf16[136,640]{1,0:T(8,128)(2,1)S(1)} %get-tuple-element.45), channel_id=1, source_target_pairs={{0,2},{1,3},{4,0},{5,1},{8,4},{9,5},{12,8},{13,9},{14,12},{15,13},... | collective-permute-start | bytes 522248 | tf_op jit(solution)/shard_map/ppermute | solution.py:39
  218.3 1.7 copy-start.7
  220.0 2.5 copy-start.9
  221.0 17.5 %collective-permute-start.27 = (bf16[264,640]{1,0:T(8,128)(2,1)S(1)}, bf16[264,640]{1,0:T(8,128)(2,1)S(1)}, u32[]{:S(2)}, u32[]{:S(2)}) collective-permute-start(bf16[264,640]{1,0:T(8,128)(2,1)S(1)} %shard_map.79), channel_id=1, source_target_pairs={{0,2},{1,3},{4,0},{5,1},{8,4},{9,5},{12,8},{13,9},{14,12},{15,13},... | collective-permute-start | bytes 1013768 | tf_op jit(solution)/shard_map/ppermute | solution.py:39
  223.5 18.3 %collective-permute-start.24 = (bf16[264,640]{1,0:T(8,128)(2,1)S(1)}, bf16[264,640]{1,0:T(8,128)(2,1)S(1)}, u32[]{:S(2)}, u32[]{:S(2)}) collective-permute-start(bf16[264,640]{1,0:T(8,128)(2,1)S(1)} %shard_map.76), channel_id=1, source_target_pairs={{0,4},{1,5},{4,8},{5,9},{8,12},{9,13},{12,14},{13,15},{14,10},{15,... | collective-permute-start | bytes 1013768 | tf_op jit(solution)/shard_map/ppermute | solution.py:39
  224.9 10.0 %collective-permute-start.33 = (bf16[136,640]{1,0:T(8,128)(2,1)S(1)}, bf16[136,640]{1,0:T(8,128)(2,1)S(1)}, u32[]{:S(2)}, u32[]{:S(2)}) collective-permute-start(bf16[136,640]{1,0:T(8,128)(2,1)S(1)} %shard_map.85), channel_id=1, source_target_pairs={{0,4},{1,5},{4,8},{5,9},{8,12},{9,13},{12,14},{13,15},{14,10},{15,... | collective-permute-start | bytes 522248 | tf_op jit(solution)/shard_map/ppermute | solution.py:39
  227.2 9.6 %collective-permute-start.30 = (bf16[136,640]{1,0:T(8,128)(2,1)S(1)}, bf16[136,640]{1,0:T(8,128)(2,1)S(1)}, u32[]{:S(2)}, u32[]{:S(2)}) collective-permute-start(bf16[136,640]{1,0:T(8,128)(2,1)S(1)} %shard_map.82), channel_id=1, source_target_pairs={{0,2},{1,3},{4,0},{5,1},{8,4},{9,5},{12,8},{13,9},{14,12},{15,13},... | collective-permute-start | bytes 522248 | tf_op jit(solution)/shard_map/ppermute | solution.py:39
  232.3 4.5 %copy-start.8 = (bf16[2048,640]{1,0:T(8,128)(2,1)S(1)}, bf16[2048,640]{1,0:T(8,128)(2,1)}, u32[]{:S(2)}) copy-start(bf16[2048,640]{1,0:T(8,128)(2,1)} %get-tuple-element.41.refs_2_) | copy-start | bytes 7864324
  235.5 3.0 %copy-start.6 = (bf16[2048,640]{1,0:T(8,128)(2,1)S(1)}, bf16[2048,640]{1,0:T(8,128)(2,1)}, u32[]{:S(2)}) copy-start(bf16[2048,640]{1,0:T(8,128)(2,1)} %get-tuple-element.42.refs_2_) | copy-start | bytes 7864324
  235.5 8.5 %collective-permute-start.34 = (bf16[136,640]{1,0:T(8,128)(2,1)S(1)}, bf16[136,640]{1,0:T(8,128)(2,1)S(1)}, u32[]{:S(2)}, u32[]{:S(2)}) collective-permute-start(bf16[136,640]{1,0:T(8,128)(2,1)S(1)} %shard_map.86), channel_id=1, source_target_pairs={{0,4},{1,5},{4,8},{5,9},{8,12},{9,13},{12,14},{13,15},{14,10},{15,... | collective-permute-start | bytes 522248 | tf_op jit(solution)/shard_map/ppermute | solution.py:39
  237.4 4.4 %copy-start.3 = (bf16[2048,640]{1,0:T(8,128)(2,1)S(1)}, bf16[2048,640]{1,0:T(8,128)(2,1)}, u32[]{:S(2)}) copy-start(bf16[2048,640]{1,0:T(8,128)(2,1)} %get-tuple-element.39.refs_2_) | copy-start | bytes 7864324
  237.4 8.9 %collective-permute-start.31 = (bf16[136,640]{1,0:T(8,128)(2,1)S(1)}, bf16[136,640]{1,0:T(8,128)(2,1)S(1)}, u32[]{:S(2)}, u32[]{:S(2)}) collective-permute-start(bf16[136,640]{1,0:T(8,128)(2,1)S(1)} %shard_map.83), channel_id=1, source_target_pairs={{0,2},{1,3},{4,0},{5,1},{8,4},{9,5},{12,8},{13,9},{14,12},{15,13},... | collective-permute-start | bytes 522248 | tf_op jit(solution)/shard_map/ppermute | solution.py:39
  240.2 13.3 %collective-permute-start.28 = (bf16[264,640]{1,0:T(8,128)(2,1)}, bf16[264,640]{1,0:T(8,128)(2,1)S(1)}, u32[]{:S(2)}, u32[]{:S(2)}) collective-permute-start(bf16[264,640]{1,0:T(8,128)(2,1)} %shard_map.80), channel_id=1, source_target_pairs={{0,2},{1,3},{4,0},{5,1},{8,4},{9,5},{12,8},{13,9},{14,12},{15,13},... | collective-permute-start | bytes 1013768 | tf_op jit(solution)/shard_map/ppermute | solution.py:39
  243.6 9.9 %collective-permute-start.25 = (bf16[264,640]{1,0:T(8,128)(2,1)}, bf16[264,640]{1,0:T(8,128)(2,1)}, u32[]{:S(2)}, u32[]{:S(2)}) collective-permute-start(bf16[264,640]{1,0:T(8,128)(2,1)} %shard_map.77), channel_id=1, source_target_pairs={{0,4},{1,5},{4,8},{5,9},{8,12},{9,13},{12,14},{13,15},{14,10},{15,... | collective-permute-start | bytes 1013768 | tf_op jit(solution)/shard_map/ppermute | solution.py:39
  245.3 8.2 %collective-permute-start.35 = (bf16[136,640]{1,0:T(8,128)(2,1)}, bf16[136,640]{1,0:T(8,128)(2,1)}, u32[]{:S(2)}, u32[]{:S(2)}) collective-permute-start(bf16[136,640]{1,0:T(8,128)(2,1)} %shard_map.87), channel_id=1, source_target_pairs={{0,4},{1,5},{4,8},{5,9},{8,12},{9,13},{12,14},{13,15},{14,10},{15,... | collective-permute-start | bytes 522248 | tf_op jit(solution)/shard_map/ppermute | solution.py:39
  247.6 5.9 %collective-permute-start.32 = (bf16[136,640]{1,0:T(8,128)(2,1)}, bf16[136,640]{1,0:T(8,128)(2,1)}, u32[]{:S(2)}, u32[]{:S(2)}) collective-permute-start(bf16[136,640]{1,0:T(8,128)(2,1)} %shard_map.84), channel_id=1, source_target_pairs={{0,2},{1,3},{4,0},{5,1},{8,4},{9,5},{12,8},{13,9},{14,12},{15,13},... | collective-permute-start | bytes 522248 | tf_op jit(solution)/shard_map/ppermute | solution.py:39
  248.6 1.7 copy-start.4
  250.3 1.7 copy-start.5
